TPU v7x, 32 devices: a whole 2x2x4 slice. The times are simulated.
32 devices in a mesh: dp: 16 (over z, y, x), mp: 2 (over core).
Axes of the slice: x: 2, y: 2, z: 4, core: 2. Of those that a mesh axis runs over, the one named last changes fastest.
Arguments:
- query: bfloat16 [1024, 4096], P('dp', 'mp'), may hold values from -144 to 144
- new_key: bfloat16 [1024, 4096], P('dp', 'mp'), may hold values from -6 to 6
- new_value: bfloat16 [1024, 4096], P('dp', 'mp'), may hold values from -6 to 6
- cache_key: bfloat16 [1024, 32, 16, 128], P('dp', 'mp'), may hold values from -6 to 6
- cache_value: bfloat16 [1024, 32, 16, 128], P('dp', 'mp'), may hold values from -6 to 6
- cache_len: int32 [1024], P('dp'), may hold values from 2 to 16
- residual: bfloat16 [1024, 8192], P('dp'), may hold values from -6 to 6
- out_weight: bfloat16 [4096, 8192], P('mp'), may hold values from -0.1875 to 0.1875
- norm_gain: bfloat16 [8192], P('mp'), may hold values from 0.25 to 1.75
- codec_weight: bfloat16 [8192, 1024], P('mp'), may hold values from -0.125 to 0.125
- finished: int32 [1024], P('dp'), may hold values from 0 to 1
- owner: int32 [1024], P('dp'), may hold values from 0 to 15, as said below
- frames: bfloat16 [16384, 1024], P('dp', 'mp'), may hold values from -6 to 6
- snake_alpha: float32 [1024], P('mp'), may hold values from 0.5 to 2
- filter_weight: bfloat16 [7, 1024, 1024], P(None, None, 'mp'), may hold values from -0.125 to 0.125
- conv_bias: float32 [1024], P('mp'), may hold values from -4 to 4
Outputs:
- hidden: bfloat16 [1024, 8192], P('dp', 'mp')
- audio: bfloat16 [16384, 1024], P('dp', 'mp')
Inputs may be any that keep to these rules, and one draw needn't show every extreme that they name: Within each aligned block of 64 rows, at most 4 finished rows name the same owner, and some owner is named by exactly 4 finished rows of the block.
All inputs are finite; a program needn't handle non-finite values.
Results may differ from a plain program's by a relative error of at most 0.0056.
Values may be sent and summed in bfloat16 or wider, within the bound.
A program may use at most 128 MiB of HBM per device.

v0:
```python
import functools
import jax
import jax.numpy as jnp
from jax import lax
from jax.experimental import pallas as pl
from jax.experimental.pallas import tpu as pltpu
from jax.sharding import PartitionSpec as P

KERNEL_TAPS = 7
DILATION_STEP = 3
CAP = 4
ROW_TILE = 16


def swap(x):
    return lax.ppermute(x, "mp", [(0, 1), (1, 0)])


def gather_mp(x, axis):
    if lax.axis_size("mp") != 2:
        return lax.all_gather(x, "mp", axis=axis, tiled=True)
    other = swap(x)
    first = lax.axis_index("mp") == 0
    return jnp.concatenate([jnp.where(first, x, other), jnp.where(first, other, x)], axis=axis)


def sin_squared(x):
    turns = jnp.round(x * 0.3183098861837907)
    r = (x - turns * 3.140625) - turns * 0.0009676535897932
    q = r * r
    p = -2.5052108e-08 + q * 1.6059044e-10
    p = 2.7557319e-06 + q * p
    p = -1.9841270e-04 + q * p
    p = 8.3333333e-03 + q * p
    p = -1.6666667e-01 + q * p
    sine = r + r * (q * p)
    return sine * sine


def snake(mix, alpha):
    return (mix + sin_squared(alpha * mix) / alpha).astype(jnp.bfloat16)


def columns_kernel(start_ref, x_ref, w_ref, o_ref):
    del start_ref
    o_ref[...] = jnp.dot(x_ref[...], w_ref[...], preferred_element_type=jnp.float32).astype(
        o_ref.dtype
    )


def columns_dot(x, w, start, width, tile, dtype):
    rows, depth = x.shape
    return pl.pallas_call(
        columns_kernel,
        out_shape=jax.ShapeDtypeStruct((rows, width), dtype),
        grid_spec=pltpu.PrefetchScalarGridSpec(
            num_scalar_prefetch=1,
            grid=(width // tile,),
            in_specs=[
                pl.BlockSpec((rows, depth), lambda j, s: (0, 0)),
                pl.BlockSpec((depth, tile), lambda j, s: (0, s[0] + j)),
            ],
            out_specs=pl.BlockSpec((rows, tile), lambda j, s: (0, j)),
        ),
        compiler_params=pltpu.CompilerParams(vmem_limit_bytes=28 * 1024 * 1024),
        cost_estimate=pl.CostEstimate(
            flops=2 * rows * depth * width, bytes_accessed=2 * depth * width, transcendentals=0
        ),
    )(jnp.full((1,), start, jnp.int32), x, w)


def handoff_kernel(
    n_dp, n_mp, near, out_ref, a_ref, b_ref, land_a, land_b, send_a, recv_a, send_b, recv_b
):
    dp = lax.axis_index("dp")
    mp = lax.axis_index("mp")
    count = n_dp * n_mp
    me = dp * n_mp + mp
    barrier = pltpu.get_barrier_semaphore()

    def place(step):
        peer = lax.rem(me + step, count)
        return peer, peer // n_mp, lax.rem(peer, n_mp)

    def greet(step, carry):
        _, pd, pm = place(step)
        pl.semaphore_signal(
            barrier, inc=1, device_id=(pd, pm), device_id_type=pl.DeviceIdType.MESH
        )
        return carry

    lax.fori_loop(1, count, greet, 0)
    pl.semaphore_wait(barrier, count - 1)

    def copy_a(pd, pm, send, recv):
        return pltpu.make_async_remote_copy(
            src_ref=out_ref.at[pd],
            dst_ref=land_a.at[me],
            send_sem=send_a.at[send],
            recv_sem=recv_a.at[recv],
            device_id=(pd, pm),
            device_id_type=pl.DeviceIdType.MESH,
        )

    def copy_b(slot, pd, pm, send, recv):
        return pltpu.make_async_remote_copy(
            src_ref=out_ref.at[pd + 1],
            dst_ref=land_b.at[slot],
            send_sem=send_b.at[send],
            recv_sem=recv_b.at[recv],
            device_id=(pd, pm),
            device_id_type=pl.DeviceIdType.MESH,
        )

    def send(step, carry):
        peer, pd, pm = place(step)
        copy_a(pd, pm, peer, me).start()
        return carry

    def send_near(step, carry):
        peer, pd, pm = place(step)
        copy_b(me, pd, pm, peer, me).start()
        return carry

    @pl.when(dp < near)
    def _():
        lax.fori_loop(1, count, send_near, 0)

    lax.fori_loop(1, count, send, 0)
    land_a[me] = out_ref[dp]

    @pl.when(dp < near)
    def _():
        land_b[me] = out_ref[dp + 1]

    def finish(step, carry):
        peer, pd, pm = place(step)
        copy = copy_a(pd, pm, peer, peer)
        copy.wait_recv()
        copy.wait_send()
        return carry

    def finish_near(step, carry):
        peer, pd, pm = place(step)
        copy_b(me, pd, pm, peer, me).wait_send()
        return carry

    def take_near(sender, carry):
        @pl.when(sender != me)
        def _():
            copy_b(sender, 0, 0, sender, sender).wait_recv()

        return carry

    lax.fori_loop(1, count, finish, 0)

    @pl.when(dp < near)
    def _():
        lax.fori_loop(1, count, finish_near, 0)

    lax.fori_loop(0, near * n_mp, take_near, 0)

    def total_of(land, first):
        total = land[first].astype(jnp.float32)
        for m in range(1, n_mp):
            total = total + land[first + m].astype(jnp.float32)
        return total

    def put(d, carry):
        a_ref[d] = total_of(land_a, d * n_mp)
        return carry

    lax.fori_loop(0, n_dp, put, 0)
    for d in range(near):
        b_ref[d] = total_of(land_b, d * n_mp)


def handoff(outgoing, near):
    n_dp, n_mp = lax.axis_size("dp"), lax.axis_size("mp")
    count = n_dp * n_mp
    _, cap, width = outgoing.shape
    vmem = pl.BlockSpec(memory_space=pltpu.VMEM)
    return pl.pallas_call(
        functools.partial(handoff_kernel, n_dp, n_mp, near),
        out_shape=(
            jax.ShapeDtypeStruct((n_dp, cap, width), jnp.float32),
            jax.ShapeDtypeStruct((near, cap, width), jnp.float32),
        ),
        in_specs=[vmem],
        out_specs=(vmem, vmem),
        scratch_shapes=[
            pltpu.VMEM((count, cap, width), jnp.bfloat16),
            pltpu.VMEM((near * n_mp, cap, width), jnp.bfloat16),
            pltpu.SemaphoreType.DMA((count,)),
            pltpu.SemaphoreType.DMA((count,)),
            pltpu.SemaphoreType.DMA((count,)),
            pltpu.SemaphoreType.DMA((near * n_mp,)),
        ],
        compiler_params=pltpu.CompilerParams(
            collective_id=0, has_side_effects=True, vmem_limit_bytes=16 * 1024 * 1024
        ),
    )(outgoing)


def round_up(n, tile):
    return -(-n // tile) * tile


def taps_of(cells, rows):
    parts = [cells[t * DILATION_STEP : t * DILATION_STEP + rows] for t in range(KERNEL_TAPS)]
    return jnp.concatenate(parts, axis=1)


def attend(query, new_key, new_value, cache_key, cache_value, cache_len):
    count, heads, positions, depth = cache_key.shape
    scale = 1.0 / jnp.sqrt(jnp.float32(depth))
    queries = query.reshape(count, heads, depth)
    fresh_key = new_key.reshape(count, heads, depth)
    fresh_value = new_value.reshape(count, heads, depth)
    scores = (
        jnp.einsum("rhd,rhld->rhl", queries, cache_key, preferred_element_type=jnp.float32) * scale
    )
    own_score = (
        jnp.einsum("rhd,rhd->rh", queries, fresh_key, preferred_element_type=jnp.float32) * scale
    )
    valid = jnp.arange(positions, dtype=jnp.int32)[None, :] < cache_len[:, None]
    scores = jnp.where(valid[:, None, :], scores, -1e30)
    top = jnp.maximum(jnp.max(scores, axis=-1), own_score)
    expo = jnp.where(valid[:, None, :], jnp.exp(scores - top[..., None]), 0.0)
    own_expo = jnp.exp(own_score - top)
    total = jnp.sum(expo, axis=-1) + own_expo
    weights = (expo / total[..., None]).astype(jnp.bfloat16)
    own_weight = (own_expo / total).astype(jnp.bfloat16)
    mixed = jnp.einsum("rhl,rhld->rhd", weights, cache_value, preferred_element_type=jnp.float32)
    mixed = mixed + own_weight.astype(jnp.float32)[..., None] * fresh_value.astype(jnp.float32)
    return mixed.astype(jnp.bfloat16).reshape(count, heads * depth)


def body(
    query,
    new_key,
    new_value,
    cache_key,
    cache_value,
    cache_len,
    residual,
    out_weight,
    norm_gain,
    codec_weight,
    finished,
    owner,
    frames,
    snake_alpha,
    filter_weight,
    conv_bias,
):
    owners = lax.axis_size("dp")
    n_mp = lax.axis_size("mp")
    core = lax.axis_index("mp")
    tally, own = frames.shape
    span = KERNEL_TAPS // 2 * DILATION_STEP
    late = owners * CAP
    near = -(-span // CAP)
    front = round_up(late + span, ROW_TILE)
    back = round_up(span, ROW_TILE)

    wide_frames = frames.astype(jnp.float32)
    alpha_all = gather_mp(snake_alpha, 0)
    early = gather_mp(snake(wide_frames, snake_alpha), 1)
    head_frames = gather_mp(frames[:late], 1)
    before = lax.ppermute(early[tally - span :], "dp", [(i, i + 1) for i in range(owners - 1)])
    after_frames = lax.ppermute(
        head_frames[: near * CAP], "dp", [(i + 1, i) for i in range(owners - 1)]
    )
    middle = tally - front - back
    main = wide_frames[front : tally - back] + conv_bias
    for t in range(KERNEL_TAPS):
        start = front - span + t * DILATION_STEP
        main = main + jnp.dot(
            early[start : start + middle], filter_weight[t], preferred_element_type=jnp.float32
        )
    main = main.astype(jnp.bfloat16)

    attended = attend(query, new_key, new_value, cache_key, cache_value, cache_len)
    count = attended.shape[0]
    width = out_weight.shape[1]
    local_width = norm_gain.shape[0]
    residual_part = lax.dynamic_slice_in_dim(residual, core * local_width, local_width, 1)
    if n_mp == 2:
        tile = 1024
        theirs = columns_dot(
            attended, out_weight, (1 - core) * (local_width // tile), local_width, tile, jnp.bfloat16
        )
        arrived = swap(theirs)
        mine = columns_dot(
            attended, out_weight, core * (local_width // tile), local_width, tile, jnp.float32
        )
        projected = mine + arrived.astype(jnp.float32)
    else:
        term = jnp.dot(attended, out_weight, preferred_element_type=jnp.float32)
        projected = lax.psum_scatter(term, "mp", scatter_dimension=1, tiled=True)
    hidden = (residual_part.astype(jnp.float32) + projected).astype(jnp.bfloat16)
    wide = hidden.astype(jnp.float32)
    squares = jnp.sum(wide * wide, axis=-1)
    squares = squares + swap(squares) if n_mp == 2 else lax.psum(squares, "mp")
    meansq = squares / width
    normed = (wide * norm_gain.astype(jnp.float32)).astype(jnp.bfloat16)
    channels = codec_weight.shape[1]
    share = columns_dot(normed, codec_weight, 0, channels, 256, jnp.float32)
    share = (share * lax.rsqrt(meansq + 1e-05)[:, None]).astype(jnp.bfloat16)

    index = jnp.arange(count, dtype=jnp.int32)
    earlier = (
        (owner[:, None] == owner[None, :])
        & (finished[None, :] == 1)
        & (index[None, :] < index[:, None])
    )
    slot = jnp.sum(earlier.astype(jnp.int32), axis=1)
    target = owner * CAP + slot
    places = jnp.arange((owners + 1) * CAP, dtype=jnp.int32)
    onehot = ((places[:, None] == target[None, :]) & (finished[None, :] == 1)).astype(jnp.bfloat16)
    outgoing = jnp.dot(onehot, share, preferred_element_type=jnp.float32).astype(jnp.bfloat16)
    here, there = handoff(outgoing.reshape(owners + 1, CAP, channels), near)
    here = here.reshape(late, channels).astype(jnp.bfloat16).astype(jnp.float32)
    there = there.reshape(near * CAP, channels).astype(jnp.bfloat16).astype(jnp.float32)

    head_mix = head_frames.astype(jnp.float32) + here
    head_act = snake(head_mix, alpha_all)
    after = snake(after_frames.astype(jnp.float32) + there, alpha_all)[:span]
    cells_a = jnp.concatenate([before, head_act, early[late : front + span]], axis=0)
    cells_b = jnp.concatenate([early[tally - back - span :], after], axis=0)
    edges = jnp.concatenate([taps_of(cells_a, front), taps_of(cells_b, back)], axis=0)
    flat = filter_weight.reshape(KERNEL_TAPS * channels, own)
    own_mix = lax.dynamic_slice_in_dim(head_mix, core * own, own, 1)
    edge_mix = jnp.concatenate(
        [own_mix, wide_frames[late:front], wide_frames[tally - back :]], axis=0
    )
    edge = jnp.dot(edges, flat, preferred_element_type=jnp.float32) + edge_mix + conv_bias
    edge = edge.astype(jnp.bfloat16)
    audio = jnp.concatenate([edge[:front], main, edge[front:]], axis=0)
    return (hidden, audio)


def solution(mesh):
    placed = (
        P("dp", "mp"),
        P("dp", "mp"),
        P("dp", "mp"),
        P("dp", "mp", None, None),
        P("dp", "mp", None, None),
        P("dp"),
        P("dp", None),
        P("mp", None),
        P("mp"),
        P("mp", None),
        P("dp"),
        P("dp"),
        P("dp", "mp"),
        P("mp"),
        P(None, None, "mp"),
        P("mp"),
    )
    return jax.shard_map(
        body, mesh=mesh, in_specs=placed, out_specs=(P("dp", "mp"), P("dp", "mp")), check_vma=False
    )
```

profile of v0, /device:TPU:0, one launch (start us, length us, event | category | flops | bytes accessed | tf_op | source)
XLA Modules:
  0.0 83.9 jit_solution(2376928151737809769)
XLA Ops:
  0.6 0.6 collective-permute-start.5
  1.2 4.0 %fusion.7 = bf16[1024,512]{1,0:T(8,128)(2,1)} fusion(f32[512]{0:T(512)} %param.29, bf16[1024,512]{1,0:T(8,128)(2,1)} %param.28), kind=kLoop, calls=%fused_computation.24 | loop fusion | flops 13631488 | bytes 2099200 | tf_op jit(solution)/shard_map/convert_element_type | solution.py:41
  5.2 0.0 collective-permute-start.1
  5.2 0.4 reshape.75
  5.6 0.0 copy-start.11
  5.6 0.0 copy-start.6
  5.7 4.5 %fusion.112 = f32[64,16,1,16]{3,2,1,0:T(1,128)S(1)} fusion(bf16[64,16,128,1]{2,3,1,0:T(2,128)(2,1)S(1)} %reshape.75, bf16[64,16,16,128]{3,2,1,0:T(8,128)(2,1)} %param.19), kind=kOutput, calls=%fused_computation.183 | convolution fusion | flops 4194304 | bytes 4521984 | tf_op jit(solution)/shard_map/rhd,rhld->rhl/dot_general | solution.py:221
  10.1 0.0 copy-start.5
  10.2 0.3 copy.20
  10.6 0.2 fusion.69
  10.8 0.1 copy.24
  10.9 0.1 fusion.88
  11.0 0.1 fusion.94
  11.1 0.5 copy.25
  11.6 0.1 copy.18
  11.7 0.1 copy.30
  11.8 3.4 %fusion.113 = f32[64,16,1,128]{3,2,1,0:T(1,128)S(1)} fusion(bf16[64,16,16,1]{2,3,1,0:T(2,128)(2,1)S(1)} %copy.25, bf16[64,16,16,128]{3,2,1,0:T(8,128)(2,1)} %param.20), kind=kOutput, calls=%fused_computation.184 | convolution fusion | flops 4194304 | bytes 4751360 | tf_op jit(solution)/shard_map/rhl,rhld->rhd/dot_general | solution.py:234
  15.2 0.2 fusion.68
  15.4 0.1 copy.33
  15.5 0.0 copy-start.1
  15.5 0.0 copy-start.12
  15.6 0.0 copy-start.10
  15.6 7.7 %shard_map.168 = bf16[64,4096]{1,0:T(8,128)(2,1)S(1)} custom-call(s32[1]{0:T(128)} %bitcast.5.start_ref, bf16[64,2048]{1,0:T(8,128)(2,1)S(1)} %bitcast.65, bf16[2048,8192]{1,0:T(8,128)(2,1)} %w_ref.4), custom_call_target="tpu_custom_call" | custom-call | flops 1073741824 | bytes 16777216 | tf_op jit(solution)/shard_map/pallas_call | solution.py:53
  23.3 0.6 collective-permute-start
  23.9 0.1 collective-permute-start.3
  24.0 0.2 convert_reduce_fusion
  24.2 7.7 %shard_map.167 = f32[64,4096]{1,0:T(8,128)S(1)} custom-call(s32[1]{0:T(128)} %bitcast.start_ref, bf16[64,2048]{1,0:T(8,128)(2,1)S(1)} %bitcast.66, bf16[2048,8192]{1,0:T(8,128)(2,1)} %w_ref.4), custom_call_target="tpu_custom_call" | custom-call | flops 1073741824 | bytes 16777216 | tf_op jit(solution)/shard_map/pallas_call | solution.py:53
  31.9 0.0 copy-start.9
  31.9 0.0 copy-start.7
  31.9 1.6 %convert_element_type.99 = f32[1024,512]{1,0:T(8,128)} convert(bf16[1024,512]{1,0:T(8,128)(2,1)S(1)} %copy-done.1) | non-fusion elementwise | flops 524288 | bytes 3145728 | tf_op jit(solution)/shard_map/convert_element_type | solution.py:267
  33.5 0.0 collective-permute-done.5
  33.6 0.0 collective-permute-done.3
  33.6 1.3 %collective-permute-start.6 = (bf16[12,1024]{1,0:T(8,128)(2,1)S(1)}, bf16[12,1024]{1,0:T(8,128)(2,1)S(1)}, u32[]{:S(2)}, u32[]{:S(2)}) collective-permute-start(bf16[12,1024]{1,0:T(8,128)(2,1)S(1)} %fusion.97), channel_id=1, source_target_pairs={{2,0},{4,2},{6,4},{8,6},{10,8},{12,10},{14,12},{16,14},{18,16},{20... | collective-permute-start | bytes 73736 | tf_op jit(solution)/shard_map/ppermute | solution.py:272
  34.9 1.5 %fusion.50 = (f32[64]{0:T(128)S(1)}, bf16[64,4096]{1,0:T(8,128)(2,1)S(1)}) fusion(f32[64,4096]{1,0:T(8,128)S(1)} %shard_map.167, bf16[64,4096]{1,0:T(8,128)(2,1)} %collective-permute-done, bf16[64,8192]{1,0:T(8,128)(2,1)} %param.22, s32[]{:T(128)S(6)} %select_n.49), kind=kLoop, calls=%fused_computation.60 | loop fusion | flops 2097088 | bytes 2621700 | tf_op jit(solution)/shard_map/reduce_sum | solution.py:304
  36.5 0.0 copy-start.3
  36.5 0.5 collective-permute-start.4
  37.0 0.1 fusion.49.x_ref
  37.1 0.0 copy-start
  37.1 3.4 %copy-done = bf16[4096,1024]{1,0:T(8,128)(2,1)S(1)} copy-done((bf16[4096,1024]{1,0:T(8,128)(2,1)S(1)}, bf16[4096,1024]{1,0:T(8,128)(2,1)}, u32[]{:S(2)}) %copy-start) | copy-done | bytes 8388632
  40.5 3.1 %shard_map.169 = f32[64,1024]{1,0:T(8,128)S(1)} custom-call(s32[1]{0:T(128)} %constant.43.clone.1.start_ref, bf16[64,4096]{1,0:T(8,128)(2,1)S(1)} %fusion.49.x_ref, bf16[4096,1024]{1,0:T(8,128)(2,1)S(1)} %copy-done), custom_call_target="tpu_custom_call" | custom-call | flops 536870912 | bytes 8388608 | tf_op jit(solution)/shard_map/pallas_call | solution.py:53
  43.7 0.0 collective-permute-done.4
  43.7 0.2 convolution_convert_fusion
  43.9 0.1 reshape.63.out_ref
  44.0 18.2 %shard_map.170 = (f32[16,4,1024]{2,1,0:T(4,128)S(1)}, f32[3,4,1024]{2,1,0:T(4,128)S(1)}) custom-call(bf16[17,4,1024]{2,1,0:T(4,128)(2,1)S(1)} %reshape.63.out_ref), custom_call_target="tpu_custom_call" | custom-call | tf_op jit(solution)/shard_map/pallas_call | solution.py:183
  62.3 0.1 reshape.66
  62.4 0.2 fusion.77
  62.7 0.1 add_multiply_fusion
  62.8 0.0 collective-permute-done.1
  62.8 0.0 slice-start
  62.8 3.3 %broadcast_select_fusion.1 = (bf16[1024,512]{1,0:T(8,128)(2,1)S(1)}, bf16[1024,512]{1,0:T(8,128)(2,1)S(1)}) fusion(bf16[1024,512]{1,0:T(8,128)(2,1)} %collective-permute-done.1, pred[]{:T(512)S(6)} %eq.17, f32[512]{0:T(512)S(1)} %copy-done.7, bf16[1024,512]{1,0:T(8,128)(2,1)S(1)} %copy-done.1), kind=kLoop, calls=%fused_computation.78 | loop fusion | flops 14680064 | bytes 4196353 | tf_op jit(solution)/shard_map/jit(_where)/select_n | solution.py:24
  66.1 0.0 slice-start.1
  66.1 2.5 %fusion.12 = f32[928,512]{1,0:T(8,128)S(1)} fusion(bf16[1024,512]{1,0:T(8,128)(2,1)S(1)} %get-tuple-element.13, bf16[1024,512]{1,0:T(8,128)(2,1)S(1)} %get-tuple-element.14, bf16[7,1024,512]{2,1,0:T(8,128)(2,1)} %param.30), kind=kOutput, calls=%fused_computation.28 | convolution fusion | flops 976879616 | bytes 5046272 | tf_op jit(solution)/shard_map/dot_general | solution.py:279
  68.7 1.1 %fusion.15 = f32[928,512]{1,0:T(8,128)S(1)} fusion(bf16[1024,512]{1,0:T(8,128)(2,1)S(1)} %get-tuple-element.13, bf16[1024,512]{1,0:T(8,128)(2,1)S(1)} %get-tuple-element.14, bf16[7,1024,512]{2,1,0:T(8,128)(2,1)S(1)} %bitcast.68), kind=kOutput, calls=%fused_computation.30 | convolution fusion | flops 976879616 | bytes 5046272 | tf_op jit(solution)/shard_map/dot_general | solution.py:279
  69.8 1.1 %fusion.18 = f32[928,512]{1,0:T(8,128)S(1)} fusion(bf16[1024,512]{1,0:T(8,128)(2,1)S(1)} %get-tuple-element.13, bf16[1024,512]{1,0:T(8,128)(2,1)S(1)} %get-tuple-element.14, bf16[7,1024,512]{2,1,0:T(8,128)(2,1)S(1)} %bitcast.68), kind=kOutput, calls=%fused_computation.32 | convolution fusion | flops 976879616 | bytes 5046272 | tf_op jit(solution)/shard_map/dot_general | solution.py:279
  71.0 1.1 %fusion.21 = f32[928,512]{1,0:T(8,128)S(1)} fusion(bf16[1024,512]{1,0:T(8,128)(2,1)S(1)} %get-tuple-element.13, bf16[1024,512]{1,0:T(8,128)(2,1)S(1)} %get-tuple-element.14, bf16[7,1024,512]{2,1,0:T(8,128)(2,1)S(1)} %bitcast.68), kind=kOutput, calls=%fused_computation.34 | convolution fusion | flops 976879616 | bytes 5046272 | tf_op jit(solution)/shard_map/dot_general | solution.py:279
  72.1 1.1 %fusion.24 = f32[928,512]{1,0:T(8,128)S(1)} fusion(bf16[1024,512]{1,0:T(8,128)(2,1)S(1)} %get-tuple-element.13, bf16[1024,512]{1,0:T(8,128)(2,1)S(1)} %get-tuple-element.14, bf16[7,1024,512]{2,1,0:T(8,128)(2,1)S(1)} %bitcast.68), kind=kOutput, calls=%fused_computation.36 | convolution fusion | flops 976879616 | bytes 5046272 | tf_op jit(solution)/shard_map/dot_general | solution.py:279
  73.3 1.1 %fusion.9 = f32[928,512]{1,0:T(8,128)S(1)} fusion(bf16[1024,512]{1,0:T(8,128)(2,1)S(1)} %get-tuple-element.13, bf16[1024,512]{1,0:T(8,128)(2,1)S(1)} %get-tuple-element.14, bf16[7,1024,512]{2,1,0:T(8,128)(2,1)S(1)} %bitcast.68), kind=kOutput, calls=%fused_computation.26 | convolution fusion | flops 976879616 | bytes 5046272 | tf_op jit(solution)/shard_map/dot_general | solution.py:279
  74.5 3.4 %collective-permute-start.2 = (bf16[9,1024]{1,0:T(8,128)(2,1)S(1)}, bf16[9,1024]{1,0:T(8,128)(2,1)S(1)}, u32[]{:S(2)}, u32[]{:S(2)}) collective-permute-start(bf16[9,1024]{1,0:T(8,128)(2,1)S(1)} %pad_maximum_fusion.10), channel_id=1, source_target_pairs={{0,2},{2,4},{4,6},{6,8},{8,10},{10,12},{12,14},{14,16},{16,18},{18... | collective-permute-start | bytes 55304 | tf_op jit(solution)/shard_map/ppermute | solution.py:271
  78.0 0.0 copy-start.8
  78.1 1.5 %copy-done.2 = f32[1024,512]{1,0:T(8,128)S(1)} copy-done((f32[1024,512]{1,0:T(8,128)S(1)}, f32[1024,512]{1,0:T(8,128)}, u32[]{:S(2)}) %copy-start.2) | copy-done | bytes 2097176
  79.6 1.6 %fusion.35 = bf16[928,512]{1,0:T(8,128)(2,1)S(1)} fusion(f32[928,512]{1,0:T(8,128)S(1)} %fusion.9, f32[928,512]{1,0:T(8,128)S(1)} %fusion.24, f32[928,512]{1,0:T(8,128)S(1)} %fusion.21, f32[928,512]{1,0:T(8,128)S(1)} %fusion.18, f32[928,512]{1,0:T(8,128)S(1)} %fusion.15, f32[928,512]{1,0:T(8,128)S(1)} %fusion.12, f32[1024,512]{1,0:T(8,128)S(1)} %copy-done.2, ...), kind=kOutput, calls=%fused_computation.48 | convolution fusion | flops 981155840 | bytes 17401856 | tf_op jit(solution)/shard_map/dot_general | solution.py:279
  81.2 0.1 pad_maximum_fusion.5
  81.5 1.3 %fusion.46 = bf16[96,512]{1,0:T(8,128)(2,1)S(1)} fusion(bf16[7168,512]{1,0:T(8,128)(2,1)S(1)} %bitcast.69, bf16[16,7168]{1,0:T(8,128)(2,1)S(1)} %slice_dynamic-update-slice_fusion.3, bf16[80,7168]{1,0:T(8,128)(2,1)S(1)} %fusion.84, f32[16,512]{1,0:T(8,128)S(1)} %get-tuple-element.18, f32[16,512]{1,0:T(8,128)S(1)} %get-tuple-element.17, ...), kind=kOutput, calls=%fused_computation.58 | convolution fusion | flops 707641344 | bytes 9013248 | tf_op jit(solution)/shard_map/dot_general | solution.py:338
  82.9 1.0 %pad_maximum_fusion.2 = bf16[1024,512]{1,0:T(8,128)(2,1)} fusion(bf16[16,512]{1,0:T(8,128)(2,1)S(1)} %slice.197, bf16[928,512]{1,0:T(8,128)(2,1)S(1)} %fusion.35, bf16[80,512]{1,0:T(8,128)(2,1)S(1)} %slice.183), kind=kLoop, calls=%fused_computation.61 | loop fusion | flops 3145728 | bytes 2097152 | tf_op jit(solution)/shard_map/concatenate | solution.py:340
  (60 shorter events, 0.8 us)
Async XLA Ops:
  0.6 4.6 %copy-start.4 = (bf16[64,2048]{1,0:T(8,128)(2,1)S(1)}, bf16[64,2048]{1,0:T(8,128)(2,1)}, u32[]{:S(2)}) copy-start(bf16[64,2048]{1,0:T(8,128)(2,1)} %param.16) | copy-start | bytes 786436
  0.6 32.9 %collective-permute-start.5 = (f32[512]{0:T(512)}, f32[512]{0:T(512)S(1)}, u32[]{:S(2)}, u32[]{:S(2)}) collective-permute-start(f32[512]{0:T(512)} %param.29), channel_id=1, source_target_pairs={{0,1},{1,0},{2,3},{3,2},{4,5},{5,4},{6,7},{7,6},{8,9},{9,8},{10,11... | collective-permute-start | bytes 6152 | tf_op jit(solution)/shard_map/ppermute | solution.py:16
  5.2 57.6 %collective-permute-start.1 = (bf16[1024,512]{1,0:T(8,128)(2,1)}, bf16[1024,512]{1,0:T(8,128)(2,1)}, u32[]{:S(2)}, u32[]{:S(2)}) collective-permute-start(bf16[1024,512]{1,0:T(8,128)(2,1)} %fusion.7), channel_id=1, source_target_pairs={{0,1},{1,0},{2,3},{3,2},{4,5},{5,4},{6,7},{7,6},{8,9},{9,8},{10,11... | collective-permute-start | bytes 3145736 | tf_op jit(solution)/shard_map/ppermute | solution.py:16
  5.6 4.8 %copy-start.11 = (s32[64]{0:T(128)S(1)}, s32[64]{0:T(128)}, u32[]{:S(2)}) copy-start(s32[64]{0:T(128)} %param.21) | copy-start | bytes 772
  5.6 4.9 %copy-start.6 = (bf16[64,2048]{1,0:T(8,128)(2,1)S(1)}, bf16[64,2048]{1,0:T(8,128)(2,1)}, u32[]{:S(2)}) copy-start(bf16[64,2048]{1,0:T(8,128)(2,1)} %param.17) | copy-start | bytes 786436
  10.1 1.5 %copy-start.5 = (bf16[64,2048]{1,0:T(8,128)(2,1)S(1)}, bf16[64,2048]{1,0:T(8,128)(2,1)}, u32[]{:S(2)}) copy-start(bf16[64,2048]{1,0:T(8,128)(2,1)} %param.18) | copy-start | bytes 786436
  15.5 8.3 %copy-start.1 = (bf16[1024,512]{1,0:T(8,128)(2,1)S(1)}, bf16[1024,512]{1,0:T(8,128)(2,1)}, u32[]{:S(2)}) copy-start(bf16[1024,512]{1,0:T(8,128)(2,1)} %param.28) | copy-start | bytes 3145732
  15.5 8.4 %copy-start.12 = (s32[64]{0:T(128)S(1)}, s32[64]{0:T(128)}, u32[]{:S(2)}) copy-start(s32[64]{0:T(128)} %param.26) | copy-start | bytes 772
  15.6 8.4 %copy-start.10 = (s32[64]{0:T(128)S(1)}, s32[64]{0:T(128)}, u32[]{:S(2)}) copy-start(s32[64]{0:T(128)} %param.27) | copy-start | bytes 772
  23.3 11.6 %collective-permute-start = (bf16[64,4096]{1,0:T(8,128)(2,1)S(1)}, bf16[64,4096]{1,0:T(8,128)(2,1)}, u32[]{:S(2)}, u32[]{:S(2)}) collective-permute-start(bf16[64,4096]{1,0:T(8,128)(2,1)S(1)} %shard_map.168), channel_id=1, source_target_pairs={{0,1},{1,0},{2,3},{3,2},{4,5},{5,4},{6,7},{7,6},{8,9},{9,8},{10,11... | collective-permute-start | bytes 1572872 | tf_op jit(solution)/shard_map/ppermute | solution.py:16
  23.9 9.7 %collective-permute-start.3 = (bf16[64,512]{1,0:T(8,128)(2,1)S(1)}, bf16[64,512]{1,0:T(8,128)(2,1)S(1)}, u32[]{:S(2)}, u32[]{:S(2)}) collective-permute-start(bf16[64,512]{1,0:T(8,128)(2,1)S(1)} %slice.126), channel_id=1, source_target_pairs={{0,1},{1,0},{2,3},{3,2},{4,5},{5,4},{6,7},{7,6},{8,9},{9,8},{10,11... | collective-permute-start | bytes 196616 | tf_op jit(solution)/shard_map/ppermute | solution.py:16
  31.9 1.7 %copy-start.9 = (bf16[4096]{0:T(1024)(128)(2,1)S(1)}, bf16[4096]{0:T(1024)(128)(2,1)}, u32[]{:S(2)}) copy-start(bf16[4096]{0:T(1024)(128)(2,1)} %param.24) | copy-start | bytes 24580
  31.9 1.7 %copy-start.7 = (f32[512]{0:T(512)S(1)}, f32[512]{0:T(512)}, u32[]{:S(2)}) copy-start(f32[512]{0:T(512)} %param.29) | copy-start | bytes 6148
  33.6 29.1 %collective-permute-start.6 = (bf16[12,1024]{1,0:T(8,128)(2,1)S(1)}, bf16[12,1024]{1,0:T(8,128)(2,1)S(1)}, u32[]{:S(2)}, u32[]{:S(2)}) collective-permute-start(bf16[12,1024]{1,0:T(8,128)(2,1)S(1)} %fusion.97), channel_id=1, source_target_pairs={{2,0},{4,2},{6,4},{8,6},{10,8},{12,10},{14,12},{16,14},{18,16},{20... | collective-permute-start | bytes 73736 | tf_op jit(solution)/shard_map/ppermute | solution.py:272
  36.5 7.2 %copy-start.3 = (bf16[64,4096]{1,0:T(8,128)(2,1)}, bf16[64,4096]{1,0:T(8,128)(2,1)S(1)}, u32[]{:S(2)}) copy-start(bf16[64,4096]{1,0:T(8,128)(2,1)S(1)} %get-tuple-element.12) | copy-start | bytes 1572868
  36.5 7.2 %collective-permute-start.4 = (f32[64]{0:T(128)S(1)}, f32[64]{0:T(128)S(1)}, u32[]{:S(2)}, u32[]{:S(2)}) collective-permute-start(f32[64]{0:T(128)S(1)} %get-tuple-element.11), channel_id=1, source_target_pairs={{0,1},{1,0},{2,3},{3,2},{4,5},{5,4},{6,7},{7,6},{8,9},{9,8},{10,11... | collective-permute-start | bytes 776 | tf_op jit(solution)/shard_map/ppermute | solution.py:16
  37.1 3.4 %copy-start = (bf16[4096,1024]{1,0:T(8,128)(2,1)S(1)}, bf16[4096,1024]{1,0:T(8,128)(2,1)}, u32[]{:S(2)}) copy-start(bf16[4096,1024]{1,0:T(8,128)(2,1)} %w_ref.5) | copy-start | bytes 25165828
  62.8 5.8 %slice-start = ((s8[7340032]{0:T(1024)(128)(4,1)}), s8[4194304]{0:T(1024)(128)(4,1)S(1)}, s32[]{:S(2)}) async-start(s8[7340032]{0:T(1024)(128)(4,1)} %bitcast.67), calls=%async_computation | async-start | bytes 8388608
  66.1 2.5 %slice-start.1 = ((s8[7340032]{0:T(1024)(128)(4,1)}), s8[3145728]{0:T(1024)(128)(4,1)S(1)}, s32[]{:S(2)}) async-start(s8[7340032]{0:T(1024)(128)(4,1)} %bitcast.67), calls=%async_computation.1 | async-start | bytes 6291456
  74.5 6.7 %collective-permute-start.2 = (bf16[9,1024]{1,0:T(8,128)(2,1)S(1)}, bf16[9,1024]{1,0:T(8,128)(2,1)S(1)}, u32[]{:S(2)}, u32[]{:S(2)}) collective-permute-start(bf16[9,1024]{1,0:T(8,128)(2,1)S(1)} %pad_maximum_fusion.10), channel_id=1, source_target_pairs={{0,2},{2,4},{4,6},{6,8},{8,10},{10,12},{12,14},{14,16},{16,18},{18... | collective-permute-start | bytes 55304 | tf_op jit(solution)/shard_map/ppermute | solution.py:271
  78.0 1.6 %copy-start.2 = (f32[1024,512]{1,0:T(8,128)S(1)}, f32[1024,512]{1,0:T(8,128)}, u32[]{:S(2)}) copy-start(f32[1024,512]{1,0:T(8,128)} %convert_element_type.99) | copy-start | bytes 6291460
  78.0 1.6 %copy-start.8 = (f32[512]{0:T(512)S(1)}, f32[512]{0:T(512)}, u32[]{:S(2)}) copy-start(f32[512]{0:T(512)} %param.31) | copy-start | bytes 6148
where the time goes:
time: 84.6 us; the launch traced here: 83.9 us
  Pallas kernels  36.8 us (43%)
  matrix products  19.3 us (23%)
  other arithmetic  13.1 us (15%)
  local copies, waits for them, and re-layouts  6.9 us (8%)
  starting transfers between devices  6.5 us (8%)
  between operations  1.36 us (2%)
    pallas_call x3, Pallas kernels, columns_dot(): pl.pallas_call(columns_kernel, out_shape=jax.ShapeDtypeStruct((rows, widt...  18.5 us
    pallas_call x1, Pallas kernels, handoff(): pl.pallas_call(functools.partial(handoff_kernel, n_dp, n_mp, near), out_s...  18.2 us
    dot_general x7, matrix products, body(): jnp.dot(early[start:start + middle], filter_weight[t], preferred_element_...  9.84 us
    unnamed x39, local copies, waits for them, and re-layouts  5.3 us
    dot_general x1, matrix products, attend(): jnp.einsum('rhd,rhld->rhl', queries, cache_key, preferred_element_type=jn...  4.48 us
    convert_element_type x3, other arithmetic, snake(): return (mix + sin_squared(alpha * mix) / alpha).astype(jnp.bfloat16)  4.24 us
    ppermute x1, starting transfers between devices, body(): lax.ppermute(early[tally - span:], 'dp', [(i, i + 1) for i in range(owner...  3.44 us
    dot_general x1, matrix products, attend(): jnp.einsum('rhl,rhld->rhd', weights, cache_value, preferred_element_type=...  3.41 us
  transfers between devices with their start and end apart: 7, of which 0 were waited for; matrix products, arithmetic and copies ran while one was open for 24% of the time, Pallas kernels for 44%

commit v1 on v0

--- a/solution.py
+++ b/solution.py
@@ -341,6 +341,787 @@
     return (hidden, audio)
 
 
+MESH = pl.DeviceIdType.MESH
+SIN_SQUARED = (
+    1.0,
+    -0.3333333134651184,
+    0.04444440081715584,
+    -0.003174516372382641,
+    0.00014100516273174435,
+    -4.2275191844964866e-06,
+    8.055603473167139e-08,
+)
+ROUNDER = 12582912.0
+
+
+def fast_snake(mix, alpha, turn, inverse):
+    turns = (mix * turn + ROUNDER) - ROUNDER
+    r = (mix * alpha - turns * 3.140625) - turns * 0.0009676535897932
+    q = r * r
+    p = SIN_SQUARED[-1] * q + SIN_SQUARED[-2]
+    for c in SIN_SQUARED[-3::-1]:
+        p = p * q + c
+    return (mix + (q * p) * inverse).astype(jnp.bfloat16)
+
+
+def iota(shape, axis):
+    return lax.broadcasted_iota(jnp.int32, shape, axis)
+
+
+def column_of(row, size):
+    spread = jnp.broadcast_to(row, (size, size))
+    return jnp.sum(
+        jnp.where(iota((size, size), 0) == iota((size, size), 1), spread, 0), axis=1, keepdims=True
+    )
+
+
+class Plan:
+    def __init__(self, query, cache_key, residual, norm_gain, codec_weight, frames):
+        self.n_dp, self.n_mp = lax.axis_size("dp"), lax.axis_size("mp")
+        self.rows, self.heads, self.positions, self.depth = cache_key.shape
+        self.width = residual.shape[1]
+        self.local = norm_gain.shape[0]
+        self.channels = codec_weight.shape[1]
+        self.tally, self.own = frames.shape
+        self.late = self.n_dp * CAP
+        self.span = KERNEL_TAPS // 2 * DILATION_STEP
+        self.near = -(-self.span // CAP)
+        self.pad = round_up(self.span, ROW_TILE)
+        self.front = round_up(self.late + self.span, ROW_TILE)
+        self.back = self.pad
+        self.middle = self.tally - self.front - self.back
+        self.chunk = 512
+        self.steps = self.local // self.chunk
+        self.slots = min(8, self.steps)
+        self.group = ROW_TILE
+        self.snake_rows = 32
+        self.send_blocks = 4
+        self.depth_in = self.heads * self.depth
+        self.unroll = 4
+
+
+def blocks_of(plan):
+    count = 4
+    unit = plan.middle // ROW_TILE
+    sizes = [(unit // count + (1 if i < unit % count else 0)) * ROW_TILE for i in range(count)]
+    starts = [plan.front + sum(sizes[:i]) for i in range(count)]
+    return list(zip(starts, sizes))
+
+
+def fused_kernel(
+    P_,
+    query,
+    new_key,
+    new_value,
+    cache_key,
+    cache_value,
+    lens,
+    residual,
+    out_weight,
+    gain,
+    codec_weight,
+    finished,
+    owner,
+    frames,
+    alpha,
+    filters,
+    bias,
+    hidden_out,
+    audio_out,
+    q_v,
+    nk_v,
+    nv_v,
+    k_v,
+    v_v,
+    len_v,
+    res_v,
+    w_v,
+    gain_raw,
+    gain_v,
+    cw_v,
+    fin_v,
+    own_v,
+    fr_v,
+    al_v,
+    fw_v,
+    bias_v,
+    act_v,
+    hf_v,
+    af_v,
+    valid_v,
+    hot_v,
+    att_v,
+    score_v,
+    p_v,
+    o_v,
+    out_v,
+    in_v,
+    hid_v,
+    acc_v,
+    sq_v,
+    sendc_v,
+    recvc_v,
+    sendh_v,
+    land_v,
+    near_v,
+    here_v,
+    there_v,
+    lhs_v,
+    audio_v,
+    s_in,
+    s_k,
+    s_v,
+    s_w,
+    s_cw,
+    s_fw,
+    s_out,
+    x_alpha,
+    x_head,
+    x_early,
+    x_before,
+    x_after,
+    x_part,
+    x_codec,
+    send_a,
+    recv_a,
+    send_b,
+    recv_b,
+):
+    n_dp, n_mp = P_.n_dp, P_.n_mp
+    count = n_dp * n_mp
+    rows, heads, positions, depth = P_.rows, P_.heads, P_.positions, P_.depth
+    chunk, steps, slots = P_.chunk, P_.steps, P_.slots
+    own, channels, tally, pad = P_.own, P_.channels, P_.tally, P_.pad
+    late, span, front, back = P_.late, P_.span, P_.front, P_.back
+    dp = lax.axis_index("dp")
+    core = lax.axis_index("mp")
+    me = dp * n_mp + core
+    other = 1 - core
+    mine_cols = pl.ds(pl.multiple_of(core * own, own), own)
+    local_cols = pl.ds(pl.multiple_of(core * P_.local, P_.local), P_.local)
+
+    def local(src, dst, sem):
+        return pltpu.make_async_copy(src, dst, sem)
+
+    def remote(src, dst, send, recv, to_dp, to_mp):
+        return pltpu.make_async_remote_copy(
+            src_ref=src,
+            dst_ref=dst,
+            send_sem=send,
+            recv_sem=recv,
+            device_id=(to_dp, to_mp),
+            device_id_type=MESH,
+        )
+
+    frames_in = local(frames, fr_v, s_in.at[0])
+    alpha_in = local(alpha, al_v.at[:, mine_cols], s_in.at[1])
+    lens_in = local(lens, len_v, s_in.at[2])
+    fin_in = local(finished, fin_v, s_in.at[3])
+    own_in = local(owner, own_v, s_in.at[4])
+    q_in = local(query, q_v, s_in.at[5])
+    nk_in = local(new_key, nk_v, s_in.at[6])
+    nv_in = local(new_value, nv_v, s_in.at[7])
+    res_in = local(residual.at[:, local_cols], res_v, s_in.at[8])
+    gain_in = local(gain, gain_raw, s_in.at[9])
+    bias_in = local(bias, bias_v, s_in.at[10])
+
+    def key_in(h):
+        return local(cache_key.at[:, h], k_v.at[h], s_k.at[h])
+
+    def value_in(h):
+        return local(cache_value.at[:, h], v_v.at[h], s_v.at[h])
+
+    def weight_in(i):
+        begin = lax.select(i < steps, other * P_.local, core * P_.local) + lax.rem(i, steps) * chunk
+        return local(
+            out_weight.at[:, pl.ds(pl.multiple_of(begin, chunk), chunk)],
+            w_v.at[lax.rem(i, slots)],
+            s_w.at[lax.rem(i, slots)],
+        )
+
+    def codec_in(i):
+        part = pl.ds(pl.multiple_of(i * chunk, chunk), chunk)
+        return local(codec_weight.at[part, :], cw_v.at[part, :], s_cw.at[i])
+
+    def filter_in(t):
+        part = pl.ds(pl.multiple_of(t * channels, channels), channels)
+        return local(filters.at[part, :], fw_v.at[part, :], s_fw.at[t])
+
+    for copy in (frames_in, alpha_in, lens_in, fin_in, own_in, q_in, nk_in, nv_in):
+        copy.start()
+
+    def start_cache(h, carry):
+        key_in(h).start()
+        value_in(h).start()
+        return carry
+
+    lax.fori_loop(0, heads, start_cache, 0)
+
+    barrier = pltpu.get_barrier_semaphore()
+
+    def place(step):
+        peer = lax.rem(me + step, count)
+        return peer, peer // n_mp, lax.rem(peer, n_mp)
+
+    def greet(step, carry):
+        _, pd, pm = place(step)
+        pl.semaphore_signal(barrier, inc=1, device_id=(pd, pm), device_id_type=MESH)
+        return carry
+
+    lax.fori_loop(1, count, greet, 0)
+
+    def start_weight(i, carry):
+        weight_in(i).start()
+        return carry
+
+    lax.fori_loop(0, slots, start_weight, 0)
+    for copy in (res_in, gain_in, bias_in):
+        copy.start()
+
+    for copy in (alpha_in, frames_in):
+        copy.wait()
+
+    my_alpha = al_v[:, mine_cols]
+    my_turn = my_alpha * 0.3183098861837907
+    my_inverse = 1.0 / my_alpha
+
+    def snake_step(i, carry):
+        part = pl.ds(pl.multiple_of(i * P_.snake_rows, P_.snake_rows), P_.snake_rows)
+        where_to = pl.ds(pl.multiple_of(pad + i * P_.snake_rows, ROW_TILE), P_.snake_rows)
+        act_v[where_to, mine_cols] = fast_snake(
+            fr_v[part, :].astype(jnp.float32), my_alpha, my_turn, my_inverse
+        )
+        return carry
+
+    lax.fori_loop(0, tally // P_.snake_rows, snake_step, 0)
+
+    pl.semaphore_wait(barrier, count - 1)
+
+    alpha_x = remote(
+        alpha, al_v.at[:, mine_cols], x_alpha.at[0], x_alpha.at[1], dp, other
+    )
+    alpha_x.start()
+    head_x = remote(frames.at[0:late], hf_v, x_head.at[0], x_head.at[1], dp, other)
+    head_x.start()
+
+    block = tally // P_.send_blocks
+
+    def early_x(b):
+        part = pl.ds(pl.multiple_of(pad + b * block, ROW_TILE), block)
+        return remote(
+            act_v.at[part, mine_cols],
+            act_v.at[part, mine_cols],
+            x_early.at[0, b],
+            x_early.at[1, b],
+            dp,
+            other,
+        )
+
+    def before_x(m, to_dp, sender):
+        cols = pl.ds(pl.multiple_of(sender * own, own), own)
+        return remote(
+            act_v.at[tally : tally + pad, mine_cols],
+            act_v.at[0:pad, cols],
+            x_before.at[0, m],
+            x_before.at[1, sender],
+            to_dp,
+            m,
+        )
+
+    def after_x(m, to_dp, sender):
+        return remote(
+            frames.at[0:pad],
+            af_v.at[sender],
+            x_after.at[0, m],
+            x_after.at[1, sender],
+            to_dp,
+            m,
+        )
+
+    for b in range(P_.send_blocks):
+        early_x(b).start()
+
+    @pl.when(dp < n_dp - 1)
+    def _():
+        for m in range(n_mp):
+            before_x(m, dp + 1, core).start()
+
+    @pl.when(dp > 0)
+    def _():
+        for m in range(n_mp):
+            after_x(m, dp - 1, core).start()
+
+    for copy in (lens_in, fin_in, own_in):
+        copy.wait()
+
+    length = column_of(len_v[...], rows)
+    lanes = P_.group * positions
+    lane = iota((rows, lanes), 1)
+    line = lax.rem(iota((rows, lanes), 0), P_.group)
+    valid = (lane // positions == line) & (lax.rem(lane, positions) < length)
+    valid_v[...] = jnp.where(valid, 0.0, -1e30)
+
+    owner_row, done_row = own_v[...], fin_v[...]
+    owner_col, done_col = column_of(owner_row, rows), column_of(done_row, rows)
+    earlier = (
+        (owner_col == owner_row)
+        & (done_col == 1)
+        & (iota((rows, rows), 0) < iota((rows, rows), 1))
+    )
+    slot = jnp.sum(jnp.where(earlier, 1, 0), axis=0, keepdims=True)
+    target = jnp.where(done_row == 1, owner_row * CAP + slot, -1)
+    hot_v[...] = jnp.where(iota((late, rows), 0) == target, 1.0, 0.0).astype(jnp.bfloat16)
+
+    for copy in (q_in, nk_in, nv_in):
+        copy.wait()
+    scale = 1.0 / jnp.sqrt(jnp.float32(depth))
+
+    def score_step(j, carry):
+        for u in range(P_.unroll):
+            key_in(j * P_.unroll + u).wait()
+        for u in range(P_.unroll):
+            h = j * P_.unroll + u
+            cols = pl.ds(pl.multiple_of(h * depth, depth), depth)
+            for g in range(rows // P_.group):
+                part = slice(g * P_.group, (g + 1) * P_.group)
+                keys = k_v[h, part].reshape(lanes, depth)
+                score_v[h, part, :] = lax.dot_general(
+                    q_v[part, cols],
+                    keys,
+                    (((1,), (1,)), ((), ())),
+                    preferred_element_type=jnp.float32,
+                )
+        return carry
+
+    lax.fori_loop(0, heads // P_.unroll, score_step, 0)
+
+    def soft_step(h, carry):
+        cols = pl.ds(pl.multiple_of(h * depth, depth), depth)
+        s = jnp.where(valid_v[...] < 0.0, -1e30, score_v[h] * scale)
+        mine = q_v[:, cols].astype(jnp.float32) * nk_v[:, cols].astype(jnp.float32)
+        mine = jnp.sum(mine, axis=1, keepdims=True) * scale
+        top = jnp.maximum(jnp.max(s, axis=1, keepdims=True), mine)
+        expo = jnp.exp(s - top)
+        mine_expo = jnp.exp(mine - top)
+        share = 1.0 / (jnp.sum(expo, axis=1, keepdims=True) + mine_expo)
+        p_v[h] = (expo * share).astype(jnp.bfloat16)
+        mine_weight = (mine_expo * share).astype(jnp.bfloat16).astype(jnp.float32)
+        o_v[h] = mine_weight * nv_v[:, cols].astype(jnp.float32)
+        return carry
+
+    lax.fori_loop(0, heads, soft_step, 0)
+
+    def value_step(j, carry):
+        for u in range(P_.unroll):
+            value_in(j * P_.unroll + u).wait()
+        for u in range(P_.unroll):
+            h = j * P_.unroll + u
+            cols = pl.ds(pl.multiple_of(h * depth, depth), depth)
+            for g in range(rows // P_.group):
+                part = slice(g * P_.group, (g + 1) * P_.group)
+                values = v_v[h, part].reshape(lanes, depth)
+                mixed = jnp.dot(p_v[h, part, :], values, preferred_element_type=jnp.float32)
+                att_v[part, cols] = (mixed + o_v[h, part, :]).astype(jnp.bfloat16)
+        return carry
+
+    lax.fori_loop(0, heads // P_.unroll, value_step, 0)
+
+    def part_x(i):
+        return remote(out_v.at[i], in_v.at[i], x_part.at[0, i], x_part.at[1, i], dp, other)
+
+    def their_step(i, carry):
+        weight_in(i).wait()
+        out_v[i] = jnp.dot(
+            att_v[...], w_v[lax.rem(i, slots)], preferred_element_type=jnp.float32
+        ).astype(jnp.bfloat16)
+        weight_in(i + slots).start()
+        codec_in(i).start()
+
+        @pl.when(i > 0)
+        def _():
+            part_x(i - 1).start()
+
+        return carry
+
+    lax.fori_loop(0, steps, their_step, 0)
+
+    def start_filter(t, carry):
+        filter_in(t).start()
+        return carry
+
+    lax.fori_loop(0, KERNEL_TAPS, start_filter, 0)
+    for copy in (res_in, gain_in, bias_in):
+        copy.wait()
+    gains = gain_raw[...].astype(jnp.float32)
+    for k in range(P_.local // 128):
+        gain_v[:, k * 128 : (k + 1) * 128] = gains[k : k + 1]
+    acc_v[...] = jnp.zeros_like(acc_v)
+    sq_v[...] = jnp.zeros_like(sq_v)
+
+    def mine_step(i, carry):
+        weight_in(i + steps).wait()
+        total = jnp.dot(att_v[...], w_v[lax.rem(i, slots)], preferred_element_type=jnp.float32)
+
+        @pl.when(i == 0)
+        def _():
+            part_x(steps - 1).start()
+
+        @pl.when(i + slots < steps)
+        def _():
+            weight_in(i + steps + slots).start()
+
+        part_x(i).wait_recv()
+        cols = pl.ds(pl.multiple_of(i * chunk, chunk), chunk)
+        total = total + in_v[i].astype(jnp.float32) + res_v[:, cols].astype(jnp.float32)
+        hidden = total.astype(jnp.bfloat16)
+        hid_v[:, cols] = hidden
+        wide = hidden.astype(jnp.float32)
+        square = wide * wide
+        squares = square[:, :128]
+        for k in range(1, chunk // 128):
+            squares = squares + square[:, k * 128 : (k + 1) * 128]
+        sq_v[...] += squares
+        normed = (wide * gain_v[:, cols]).astype(jnp.bfloat16)
+        codec_in(i).wait()
+        acc_v[...] += jnp.dot(normed, cw_v[cols, :], preferred_element_type=jnp.float32)
+        return carry
+
+    lax.fori_loop(0, steps, mine_step, 0)
+    hidden_x = local(hid_v, hidden_out, s_out.at[0])
+    hidden_x.start()
+
+    other_cols = pl.ds(pl.multiple_of(other * own, own), own)
+    sendc_v[:, :own] = acc_v[:, other_cols]
+    sendc_v[:, own:] = sq_v[...]
+    codec_x = remote(sendc_v, recvc_v, x_codec.at[0], x_codec.at[1], dp, other)
+    codec_x.start()
+
+    def wait_filter(t, carry):
+        filter_in(t).wait()
+        return carry
+
+    lax.fori_loop(0, KERNEL_TAPS, wait_filter, 0)
+    for b in range(P_.send_blocks):
+        early_x(b).wait_recv()
+
+    def conv_block(index):
+        begin, size = blocks_of(P_)[index]
+        for t in range(KERNEL_TAPS):
+            at = pad + begin - span + t * DILATION_STEP
+            lhs_v[:size, t * channels : (t + 1) * channels] = act_v[at : at + size, :]
+        audio_v[begin : begin + size, :] = (
+            jnp.dot(lhs_v[:size, :], fw_v[...], preferred_element_type=jnp.float32)
+            + fr_v[begin : begin + size, :].astype(jnp.float32)
+            + bias_v[...]
+        ).astype(jnp.bfloat16)
+
+    conv_block(0)
+    codec_x.wait_recv()
+    square = jnp.sum(sq_v[...] + recvc_v[:, own:], axis=1, keepdims=True)
+    latent = (
+        (acc_v[:, mine_cols] + recvc_v[:, :own]) * lax.rsqrt(square / P_.width + 1e-05)
+    ).astype(jnp.bfloat16)
+    outgoing = jnp.dot(hot_v[...], latent, preferred_element_type=jnp.float32)
+    for d in range(n_dp):
+        sendh_v[d] = outgoing[d * CAP : (d + 1) * CAP].astype(jnp.bfloat16)
+
+    def copy_a(pd, pm, src_dp, src_mp, send, recv):
+        return remote(
+            sendh_v.at[pd], land_v.at[src_mp, src_dp], send_a.at[send], recv_a.at[recv], pd, pm
+        )
+
+    def copy_b(pd, pm, src_dp, src_mp, send, recv):
+        return remote(
+            sendh_v.at[pd + 1], near_v.at[src_mp, src_dp], send_b.at[send], recv_b.at[recv], pd, pm
+        )
+
+    def send_near(step, carry):
+        peer, pd, pm = place(step)
+
+        @pl.when(pd < n_dp - 1)
+        def _():
+            copy_b(pd, pm, dp, core, peer, me).start()
+
+        return carry
+
+    @pl.when(dp < P_.near)
+    def _():
+        lax.fori_loop(1, count, send_near, 0)
+
+    def send(step, carry):
+        peer, pd, pm = place(step)
+        copy_a(pd, pm, dp, core, peer, me).start()
+        return carry
+
+    lax.fori_loop(1, count, send, 0)
+    land_v[core, dp] = sendh_v[dp]
+
+    @pl.when(dp < P_.near)
+    def _():
+        near_v[core, dp] = sendh_v[lax.rem(dp + 1, n_dp)]
+
+    for index in range(1, len(blocks_of(P_))):
+        conv_block(index)
+    middle_x = local(
+        audio_v.at[front : tally - back], audio_out.at[front : tally - back], s_out.at[1]
+    )
+    middle_x.start()
+
+    alpha_x.wait_recv()
+    head_x.wait_recv()
+
+    def finish(step, carry):
+        peer, pd, pm = place(step)
+        copy_a(pd, pm, pd, pm, peer, peer).wait_recv()
+        return carry
+
+    lax.fori_loop(1, count, finish, 0)
+    for s in range(n_dp):
+        for m in range(n_mp):
+            here_v[s * CAP : (s + 1) * CAP, m * own : (m + 1) * own] = land_v[m, s].astype(
+                jnp.float32
+            )
+    for b in range(P_.send_blocks):
+        early_x(b).wait_send()
+    hf = hf_v[...].astype(jnp.float32)
+    mf = fr_v[0:late, :].astype(jnp.float32)
+
+    all_alpha = al_v[...]
+    all_turn = all_alpha * 0.3183098861837907
+    all_inverse = 1.0 / all_alpha
+    here_v[:, mine_cols] += mf
+    here_v[:, other_cols] += hf
+    act_v[pad : pad + late, :] = fast_snake(here_v[...], all_alpha, all_turn, all_inverse)
+
+    @pl.when(dp < n_dp - 1)
+    def _():
+        for m in range(n_mp):
+            after_x(0, 0, m).wait_recv()
+
+        def take_near(sender, carry):
+            @pl.when(sender != me)
+            def _():
+                copy_b(0, 0, sender // n_mp, lax.rem(sender, n_mp), 0, sender).wait_recv()
+
+            return carry
+
+        lax.fori_loop(0, P_.near * n_mp, take_near, 0)
+        for m in range(n_mp):
+            there_v[:, m * own : (m + 1) * own] = af_v[m].astype(jnp.float32)
+            for s in range(P_.near):
+                there_v[s * CAP : (s + 1) * CAP, m * own : (m + 1) * own] += near_v[m, s].astype(
+                    jnp.float32
+                )
+        act_v[pad + tally :, :] = fast_snake(there_v[...], all_alpha, all_turn, all_inverse)
+
+    @pl.when(dp == n_dp - 1)
+    def _():
+        act_v[pad + tally :, :] = jnp.zeros((pad, channels), jnp.bfloat16)
+
+    @pl.when(dp > 0)
+    def _():
+        for m in range(n_mp):
+            before_x(0, 0, m).wait_recv()
+
+    @pl.when(dp == 0)
+    def _():
+        act_v[0:pad, :] = jnp.zeros((pad, channels), jnp.bfloat16)
+
+    for t in range(KERNEL_TAPS):
+        cols = slice(t * channels, (t + 1) * channels)
+        at = pad - span + t * DILATION_STEP
+        lhs_v[:front, cols] = act_v[at : at + front, :]
+        at = at + tally - back
+        lhs_v[front : front + back, cols] = act_v[at : at + back, :]
+    edge = (
+        jnp.dot(lhs_v[: front + back, :], fw_v[...], preferred_element_type=jnp.float32)
+        + bias_v[...]
+    )
+    audio_v[:late, :] = (edge[:late] + here_v[:, mine_cols]).astype(jnp.bfloat16)
+    audio_v[late:front, :] = (edge[late:front] + fr_v[late:front, :].astype(jnp.float32)).astype(
+        jnp.bfloat16
+    )
+    audio_v[tally - back :, :] = (edge[front:] + fr_v[tally - back :, :].astype(jnp.float32)).astype(
+        jnp.bfloat16
+    )
+    first_x = local(audio_v.at[:front], audio_out.at[:front], s_out.at[2])
+    last_x = local(audio_v.at[tally - back :], audio_out.at[tally - back :], s_out.at[3])
+    first_x.start()
+    last_x.start()
+
+    alpha_x.wait_send()
+    head_x.wait_send()
+
+    @pl.when(dp < n_dp - 1)
+    def _():
+        for m in range(n_mp):
+            before_x(m, 0, core).wait_send()
+
+    @pl.when(dp > 0)
+    def _():
+        for m in range(n_mp):
+            after_x(m, 0, core).wait_send()
+
+    def part_sent(i, carry):
+        part_x(i).wait_send()
+        return carry
+
+    lax.fori_loop(0, steps, part_sent, 0)
+    codec_x.wait_send()
+
+    def sent(step, carry):
+        peer, pd, pm = place(step)
+        copy_a(pd, pm, dp, core, peer, me).wait_send()
+        return carry
+
+    lax.fori_loop(1, count, sent, 0)
+
+    def sent_near(step, carry):
+        peer, pd, pm = place(step)
+
+        @pl.when(pd < n_dp - 1)
+        def _():
+            copy_b(pd, pm, dp, core, peer, me).wait_send()
+
+        return carry
+
+    @pl.when(dp < P_.near)
+    def _():
+        lax.fori_loop(1, count, sent_near, 0)
+
+    hidden_x.wait()
+    middle_x.wait()
+    first_x.wait()
+    last_x.wait()
+
+
+def fused(
+    query,
+    new_key,
+    new_value,
+    cache_key,
+    cache_value,
+    cache_len,
+    residual,
+    out_weight,
+    norm_gain,
+    codec_weight,
+    finished,
+    owner,
+    frames,
+    snake_alpha,
+    filter_weight,
+    conv_bias,
+):
+    plan = Plan(query, cache_key, residual, norm_gain, codec_weight, frames)
+    n_dp, n_mp = plan.n_dp, plan.n_mp
+    count = n_dp * n_mp
+    bf, f32, i32 = jnp.bfloat16, jnp.float32, jnp.int32
+    vm = pltpu.VMEM
+    dma = pltpu.SemaphoreType.DMA
+    rows, own, channels, tally = plan.rows, plan.own, plan.channels, plan.tally
+    taps = KERNEL_TAPS * channels
+    biggest = max([size for _, size in blocks_of(plan)] + [plan.front + plan.back])
+    scratch = [
+        vm(query.shape, bf),
+        vm(query.shape, bf),
+        vm(query.shape, bf),
+        vm((plan.heads, rows, plan.positions, plan.depth), bf),
+        vm((plan.heads, rows, plan.positions, plan.depth), bf),
+        vm((1, rows), i32),
+        vm((rows, plan.local), bf),
+        vm((plan.slots, plan.depth_in, plan.chunk), bf),
+        vm((plan.local // 128, 128), bf),
+        vm((1, plan.local), f32),
+        vm((plan.local, channels), bf),
+        vm((1, rows), i32),
+        vm((1, rows), i32),
+        vm((tally, own), bf),
+        vm((1, channels), f32),
+        vm((taps, own), bf),
+        vm((1, own), f32),
+        vm((tally + 2 * plan.pad, channels), bf),
+        vm((plan.late, own), bf),
+        vm((n_mp, plan.pad, own), bf),
+        vm((rows, plan.group * plan.positions), f32),
+        vm((plan.late, rows), bf),
+        vm((rows, plan.depth_in), bf),
+        vm((plan.heads, rows, plan.group * plan.positions), f32),
+        vm((plan.heads, rows, plan.group * plan.positions), bf),
+        vm((plan.heads, rows, plan.depth), f32),
+        vm((plan.steps, rows, plan.chunk), bf),
+        vm((plan.steps, rows, plan.chunk), bf),
+        vm((rows, plan.local), bf),
+        vm((rows, channels), f32),
+        vm((rows, 128), f32),
+        vm((rows, own + 128), f32),
+        vm((rows, own + 128), f32),
+        vm((n_dp, CAP, own), bf),
+        vm((n_mp, n_dp, CAP, own), bf),
+        vm((n_mp, plan.near, CAP, own), bf),
+        vm((plan.late, channels), f32),
+        vm((plan.pad, channels), f32),
+        vm((biggest, taps), bf),
+        vm((tally, own), bf),
+        dma((11,)),
+        dma((plan.heads,)),
+        dma((plan.heads,)),
+        dma((plan.slots,)),
+        dma((plan.steps,)),
+        dma((KERNEL_TAPS,)),
+        dma((4,)),
+        dma((2,)),
+        dma((2,)),
+        dma((2, plan.send_blocks)),
+        dma((2, n_mp)),
+        dma((2, n_mp)),
+        dma((2, plan.steps)),
+        dma((2,)),
+        dma((count,)),
+        dma((count,)),
+        dma((count,)),
+        dma((plan.near * n_mp,)),
+    ]
+    anywhere = pl.BlockSpec(memory_space=pl.ANY)
+    return pl.pallas_call(
+        functools.partial(fused_kernel, plan),
+        out_shape=(
+            jax.ShapeDtypeStruct((rows, plan.local), bf),
+            jax.ShapeDtypeStruct((tally, own), bf),
+        ),
+        in_specs=[anywhere] * 16,
+        out_specs=(anywhere, anywhere),
+        scratch_shapes=scratch,
+        compiler_params=pltpu.CompilerParams(
+            collective_id=1, has_side_effects=True, vmem_limit_bytes=VMEM_BYTES
+        ),
+    )(
+        query,
+        new_key,
+        new_value,
+        cache_key,
+        cache_value,
+        cache_len.reshape(1, -1),
+        residual,
+        out_weight,
+        norm_gain.reshape(-1, 128),
+        codec_weight,
+        finished.reshape(1, -1),
+        owner.reshape(1, -1),
+        frames,
+        snake_alpha.reshape(1, -1),
+        filter_weight.reshape(taps, own),
+        conv_bias.reshape(1, -1),
+    )
+
+
+VMEM_BYTES = 66 * 1000 * 1000
+
+
+def step(*args):
+    return fused(*args) if lax.axis_size("mp") == 2 else body(*args)
+
+
 def solution(mesh):
     placed = (
         P("dp", "mp"),
@@ -361,5 +1142,5 @@
         P("mp"),
     )
     return jax.shard_map(
-        body, mesh=mesh, in_specs=placed, out_specs=(P("dp", "mp"), P("dp", "mp")), check_vma=False
-    )
+        step, mesh=mesh, in_specs=placed, out_specs=(P("dp", "mp"), P("dp", "mp")), check_vma=False
+    )

time: 84.6 us -> 43.5 us (0.51)
  matrix products: 19.3 us -> 0 us
  other arithmetic: 13.1 us -> 0 us
  starting transfers between devices: 6.5 us -> 0 us
  local copies, waits for them, and re-layouts: 6.9 us -> 4.13 us
  Pallas kernels: 36.8 us -> 38.5 us
    dot_general x11 -> x0, matrix products: 19.3 us -> none  [the longest x7 9.84 us: body(): jnp.dot(early[start:start + middle], filter_weight[t], preferred_element_...]
    ppermute x7 -> x0, starting transfers between devices: 6.5 us -> none  [the longest x1 3.44 us: body(): lax.ppermute(early[tally - span:], 'dp', [(i, i + 1) for i in range(owner...]
    convert_element_type x11 -> x0, other arithmetic: 6.26 us -> none  [the longest x3 4.24 us: snake(): return (mix + sin_squared(alpha * mix) / alpha).astype(jnp.bfloat16)]
    select_n x3 -> x0, other arithmetic: 3.31 us -> none  [the longest x2 3.3 us: gather_mp(): jnp.where(first, x, other)]
    pallas_call x4 -> x1, Pallas kernels: 36.8 us -> 38.5 us  [fused(): pl.pallas_call(functools.partial(fused_kernel, plan), out_shape=(jax.Shap...]
    reduce_sum x3 -> x0, other arithmetic: 1.77 us -> none  [the longest x1 1.53 us: body(): squares = jnp.sum(wide * wide, axis=-1)]
    concatenate x6 -> x0, other arithmetic: 1.19 us -> none  [the longest x1 1.04 us: body(): audio = jnp.concatenate([edge[:front], main, edge[front:]], axis=0)]
    unnamed x39 -> x2, local copies, waits for them, and re-layouts: 5.3 us -> 4.13 us
  transfers between devices with their start and end apart: 7 -> 0, of which waited for: 0 -> 0; matrix products, arithmetic and copies ran while one was open for 24% -> 0% of each run, Pallas kernels for 44% -> 0%
where the time goes in v1:
time: 43.5 us; the launch traced here: 43.3 us
  Pallas kernels  38.5 us (89%)
  local copies, waits for them, and re-layouts  4.13 us (9%)
  between operations  0.65 us (1%)
    pallas_call x1, Pallas kernels, fused(): pl.pallas_call(functools.partial(fused_kernel, plan), out_shape=(jax.Shap...  38.5 us
    unnamed x2, local copies, waits for them, and re-layouts  4.13 us

profile of v1, /device:TPU:0, one launch (start us, length us, event | category | flops | bytes accessed | tf_op | source)
XLA Modules:
  0.0 43.3 jit_solution(8663276278629783875)
XLA Ops:
  0.6 38.5 %shard_map.167 = (bf16[64,4096]{1,0:T(8,128)(2,1)}, bf16[1024,512]{1,0:T(8,128)(2,1)}) custom-call(bf16[64,2048]{1,0:T(8,128)(2,1)} %query.1, bf16[64,2048]{1,0:T(8,128)(2,1)} %new_key.1, bf16[64,2048]{1,0:T(8,128)(2,1)} %new_value.1, bf16[64,16,16,128]{3,2,1,0:T(8,128)(2,1)} %cache_key.1, bf16[64,16,16,128]{3,2,1,0:T(8,128)(2,1)} %cache_value.1, ...), custom_call_target="tpu_custom_call" | custom-call | tf_op jit(solution)/shard_map/pallas_call | solution.py:1086
  39.2 1.9 %copy.20 = bf16[64,4096]{1,0:T(8,128)(2,1)} copy(bf16[64,4096]{1,0:T(8,128)(2,1)} %get-tuple-element.4) | data formatting | bytes 1048576
  41.1 2.3 %copy.21 = bf16[1024,512]{1,0:T(8,128)(2,1)} copy(bf16[1024,512]{1,0:T(8,128)(2,1)} %get-tuple-element.5) | data formatting | bytes 2097152

commit v2 on v1

--- a/solution.py
+++ b/solution.py
@@ -436,6 +436,7 @@
     len_v,
     res_v,
     w_v,
+    normed_v,
     gain_raw,
     gain_v,
     cw_v,
@@ -547,15 +548,21 @@
         part = pl.ds(pl.multiple_of(t * channels, channels), channels)
         return local(filters.at[part, :], fw_v.at[part, :], s_fw.at[t])
 
-    for copy in (frames_in, alpha_in, lens_in, fin_in, own_in, q_in, nk_in, nv_in):
+    for copy in (lens_in, q_in, nk_in):
         copy.start()
 
-    def start_cache(h, carry):
+    def start_key(h, carry):
         key_in(h).start()
+        return carry
+
+    def start_value(h, carry):
         value_in(h).start()
         return carry
 
-    lax.fori_loop(0, heads, start_cache, 0)
+    lax.fori_loop(0, heads, start_key, 0)
+    lax.fori_loop(0, heads, start_value, 0)
+    for copy in (nv_in, alpha_in, fin_in, own_in, frames_in):
+        copy.start()
 
     barrier = pltpu.get_barrier_semaphore()
 
@@ -578,78 +585,11 @@
     for copy in (res_in, gain_in, bias_in):
         copy.start()
 
-    for copy in (alpha_in, frames_in):
-        copy.wait()
-
-    my_alpha = al_v[:, mine_cols]
-    my_turn = my_alpha * 0.3183098861837907
-    my_inverse = 1.0 / my_alpha
-
-    def snake_step(i, carry):
-        part = pl.ds(pl.multiple_of(i * P_.snake_rows, P_.snake_rows), P_.snake_rows)
-        where_to = pl.ds(pl.multiple_of(pad + i * P_.snake_rows, ROW_TILE), P_.snake_rows)
-        act_v[where_to, mine_cols] = fast_snake(
-            fr_v[part, :].astype(jnp.float32), my_alpha, my_turn, my_inverse
-        )
-        return carry
-
-    lax.fori_loop(0, tally // P_.snake_rows, snake_step, 0)
-
-    pl.semaphore_wait(barrier, count - 1)
-
-    alpha_x = remote(
-        alpha, al_v.at[:, mine_cols], x_alpha.at[0], x_alpha.at[1], dp, other
-    )
-    alpha_x.start()
-    head_x = remote(frames.at[0:late], hf_v, x_head.at[0], x_head.at[1], dp, other)
-    head_x.start()
-
-    block = tally // P_.send_blocks
-
-    def early_x(b):
-        part = pl.ds(pl.multiple_of(pad + b * block, ROW_TILE), block)
-        return remote(
-            act_v.at[part, mine_cols],
-            act_v.at[part, mine_cols],
-            x_early.at[0, b],
-            x_early.at[1, b],
-            dp,
-            other,
-        )
-
-    def before_x(m, to_dp, sender):
-        cols = pl.ds(pl.multiple_of(sender * own, own), own)
-        return remote(
-            act_v.at[tally : tally + pad, mine_cols],
-            act_v.at[0:pad, cols],
-            x_before.at[0, m],
-            x_before.at[1, sender],
-            to_dp,
-            m,
-        )
-
-    def after_x(m, to_dp, sender):
-        return remote(
-            frames.at[0:pad],
-            af_v.at[sender],
-            x_after.at[0, m],
-            x_after.at[1, sender],
-            to_dp,
-            m,
-        )
-
-    for b in range(P_.send_blocks):
-        early_x(b).start()
-
-    @pl.when(dp < n_dp - 1)
-    def _():
-        for m in range(n_mp):
-            before_x(m, dp + 1, core).start()
-
-    @pl.when(dp > 0)
-    def _():
-        for m in range(n_mp):
-            after_x(m, dp - 1, core).start()
+    def start_codec(i, carry):
+        codec_in(i).start()
+        return carry
+
+    lax.fori_loop(0, steps, start_codec, 0)
 
     for copy in (lens_in, fin_in, own_in):
         copy.wait()
@@ -726,24 +666,94 @@
 
     lax.fori_loop(0, heads // P_.unroll, value_step, 0)
 
+    alpha_x = remote(
+        alpha, al_v.at[:, mine_cols], x_alpha.at[0], x_alpha.at[1], dp, other
+    )
+    head_x = remote(frames.at[0:late], hf_v, x_head.at[0], x_head.at[1], dp, other)
+
+    block = tally // P_.send_blocks
+
+    def early_x(b):
+        part = pl.ds(pl.multiple_of(pad + b * block, ROW_TILE), block)
+        return remote(
+            act_v.at[part, mine_cols],
+            act_v.at[part, mine_cols],
+            x_early.at[0, b],
+            x_early.at[1, b],
+            dp,
+            other,
+        )
+
+    def before_x(m, to_dp, sender):
+        cols = pl.ds(pl.multiple_of(sender * own, own), own)
+        return remote(
+            act_v.at[tally : tally + pad, mine_cols],
+            act_v.at[0:pad, cols],
+            x_before.at[0, m],
+            x_before.at[1, sender],
+            to_dp,
+            m,
+        )
+
+    def after_x(m, to_dp, sender):
+        return remote(
+            frames.at[0:pad],
+            af_v.at[sender],
+            x_after.at[0, m],
+            x_after.at[1, sender],
+            to_dp,
+            m,
+        )
+
+    pl.semaphore_wait(barrier, count - 1)
+    alpha_x.start()
+    head_x.start()
+
+    @pl.when(dp > 0)
+    def _():
+        for m in range(n_mp):
+            after_x(m, dp - 1, core).start()
+
+    for copy in (alpha_in, frames_in):
+        copy.wait()
+    my_alpha = al_v[:, mine_cols]
+    my_turn = my_alpha * 0.3183098861837907
+    my_inverse = 1.0 / my_alpha
+    snake_rows = tally // steps
+
     def part_x(i):
         return remote(out_v.at[i], in_v.at[i], x_part.at[0, i], x_part.at[1, i], dp, other)
 
     def their_step(i, carry):
+        @pl.when(i > 0)
+        def _():
+            part_x(i - 1).start()
+
         weight_in(i).wait()
+        for k in range(snake_rows // P_.snake_rows):
+            begin = i * snake_rows + k * P_.snake_rows
+            part = pl.ds(pl.multiple_of(begin, P_.snake_rows), P_.snake_rows)
+            where_to = pl.ds(pl.multiple_of(pad + begin, ROW_TILE), P_.snake_rows)
+            act_v[where_to, mine_cols] = fast_snake(
+                fr_v[part, :].astype(jnp.float32), my_alpha, my_turn, my_inverse
+            )
         out_v[i] = jnp.dot(
             att_v[...], w_v[lax.rem(i, slots)], preferred_element_type=jnp.float32
         ).astype(jnp.bfloat16)
         weight_in(i + slots).start()
-        codec_in(i).start()
-
-        @pl.when(i > 0)
-        def _():
-            part_x(i - 1).start()
-
         return carry
 
     lax.fori_loop(0, steps, their_step, 0)
+    part_x(steps - 1).start()
+
+    for b in range(P_.send_blocks):
+        early_x(b).start()
+
+    @pl.when(dp < n_dp - 1)
+    def _():
+        for m in range(n_mp):
+            before_x(m, dp + 1, core).start()
+
 
     def start_filter(t, carry):
         filter_in(t).start()
@@ -758,20 +768,9 @@
     acc_v[...] = jnp.zeros_like(acc_v)
     sq_v[...] = jnp.zeros_like(sq_v)
 
-    def mine_step(i, carry):
-        weight_in(i + steps).wait()
+    def produce(i):
+        cols = pl.ds(pl.multiple_of(i * chunk, chunk), chunk)
         total = jnp.dot(att_v[...], w_v[lax.rem(i, slots)], preferred_element_type=jnp.float32)
-
-        @pl.when(i == 0)
-        def _():
-            part_x(steps - 1).start()
-
-        @pl.when(i + slots < steps)
-        def _():
-            weight_in(i + steps + slots).start()
-
-        part_x(i).wait_recv()
-        cols = pl.ds(pl.multiple_of(i * chunk, chunk), chunk)
         total = total + in_v[i].astype(jnp.float32) + res_v[:, cols].astype(jnp.float32)
         hidden = total.astype(jnp.bfloat16)
         hid_v[:, cols] = hidden
@@ -781,12 +780,33 @@
         for k in range(1, chunk // 128):
             squares = squares + square[:, k * 128 : (k + 1) * 128]
         sq_v[...] += squares
-        normed = (wide * gain_v[:, cols]).astype(jnp.bfloat16)
-        codec_in(i).wait()
-        acc_v[...] += jnp.dot(normed, cw_v[cols, :], preferred_element_type=jnp.float32)
-        return carry
-
-    lax.fori_loop(0, steps, mine_step, 0)
+        normed_v[lax.rem(i, 2)] = (wide * gain_v[:, cols]).astype(jnp.bfloat16)
+
+    def consume(i):
+        cols = pl.ds(pl.multiple_of(i * chunk, chunk), chunk)
+        acc_v[...] += jnp.dot(
+            normed_v[lax.rem(i, 2)], cw_v[cols, :], preferred_element_type=jnp.float32
+        )
+
+    def mine_step(i, carry):
+        codec_in(i - 1).wait()
+        weight_in(i + steps).wait()
+        part_x(i).wait_recv()
+        consume(i - 1)
+        produce(i)
+
+        @pl.when(i + slots < steps)
+        def _():
+            weight_in(i + steps + slots).start()
+
+        return carry
+
+    weight_in(jnp.int32(steps)).wait()
+    part_x(0).wait_recv()
+    produce(jnp.int32(0))
+    lax.fori_loop(1, steps, mine_step, 0)
+    codec_in(steps - 1).wait()
+    consume(jnp.int32(steps - 1))
     hidden_x = local(hid_v, hidden_out, s_out.at[0])
     hidden_x.start()
 
@@ -795,14 +815,6 @@
     sendc_v[:, own:] = sq_v[...]
     codec_x = remote(sendc_v, recvc_v, x_codec.at[0], x_codec.at[1], dp, other)
     codec_x.start()
-
-    def wait_filter(t, carry):
-        filter_in(t).wait()
-        return carry
-
-    lax.fori_loop(0, KERNEL_TAPS, wait_filter, 0)
-    for b in range(P_.send_blocks):
-        early_x(b).wait_recv()
 
     def conv_block(index):
         begin, size = blocks_of(P_)[index]
@@ -815,7 +827,6 @@
             + bias_v[...]
         ).astype(jnp.bfloat16)
 
-    conv_block(0)
     codec_x.wait_recv()
     square = jnp.sum(sq_v[...] + recvc_v[:, own:], axis=1, keepdims=True)
     latent = (
@@ -844,23 +855,32 @@
 
         return carry
 
-    @pl.when(dp < P_.near)
-    def _():
-        lax.fori_loop(1, count, send_near, 0)
-
     def send(step, carry):
         peer, pd, pm = place(step)
         copy_a(pd, pm, dp, core, peer, me).start()
         return carry
 
     lax.fori_loop(1, count, send, 0)
+
+    @pl.when(dp < P_.near)
+    def _():
+        lax.fori_loop(1, count, send_near, 0)
+
     land_v[core, dp] = sendh_v[dp]
 
     @pl.when(dp < P_.near)
     def _():
         near_v[core, dp] = sendh_v[lax.rem(dp + 1, n_dp)]
 
-    for index in range(1, len(blocks_of(P_))):
+    def wait_filter(t, carry):
+        filter_in(t).wait()
+        return carry
+
+    lax.fori_loop(0, KERNEL_TAPS, wait_filter, 0)
+    for b in range(P_.send_blocks):
+        early_x(b).wait_recv()
+
+    for index in range(len(blocks_of(P_))):
         conv_block(index)
     middle_x = local(
         audio_v.at[front : tally - back], audio_out.at[front : tally - back], s_out.at[1]
@@ -1031,6 +1051,7 @@
         vm((1, rows), i32),
         vm((rows, plan.local), bf),
         vm((plan.slots, plan.depth_in, plan.chunk), bf),
+        vm((2, rows, plan.chunk), bf),
         vm((plan.local // 128, 128), bf),
         vm((1, plan.local), f32),
         vm((plan.local, channels), bf),

time: 43.5 us -> 40.3 us (0.926)
  Pallas kernels: 38.5 us -> 35.1 us
    pallas_call x1, Pallas kernels: 38.5 us -> 35.1 us  [fused(): pl.pallas_call(functools.partial(fused_kernel, plan), out_shape=(jax.Shap...]
where the time goes in v2:
time: 40.3 us; the launch traced here: 39.9 us
  Pallas kernels  35.1 us (87%)
  local copies, waits for them, and re-layouts  4.13 us (10%)
  between operations  0.65 us (2%)
    pallas_call x1, Pallas kernels, fused(): pl.pallas_call(functools.partial(fused_kernel, plan), out_shape=(jax.Shap...  35.1 us
    unnamed x2, local copies, waits for them, and re-layouts  4.13 us

profile of v2, /device:TPU:0, one launch (start us, length us, event | category | flops | bytes accessed | tf_op | source)
XLA Modules:
  0.0 39.9 jit_solution(6170664594233808501)
XLA Ops:
  0.6 35.1 %shard_map.167 = (bf16[64,4096]{1,0:T(8,128)(2,1)}, bf16[1024,512]{1,0:T(8,128)(2,1)}) custom-call(bf16[64,2048]{1,0:T(8,128)(2,1)} %query.1, bf16[64,2048]{1,0:T(8,128)(2,1)} %new_key.1, bf16[64,2048]{1,0:T(8,128)(2,1)} %new_value.1, bf16[64,16,16,128]{3,2,1,0:T(8,128)(2,1)} %cache_key.1, bf16[64,16,16,128]{3,2,1,0:T(8,128)(2,1)} %cache_value.1, ...), custom_call_target="tpu_custom_call" | custom-call | tf_op jit(solution)/shard_map/pallas_call | solution.py:1107
  35.7 1.9 %copy.20 = bf16[64,4096]{1,0:T(8,128)(2,1)} copy(bf16[64,4096]{1,0:T(8,128)(2,1)} %get-tuple-element.4) | data formatting | bytes 1048576
  37.6 2.3 %copy.21 = bf16[1024,512]{1,0:T(8,128)(2,1)} copy(bf16[1024,512]{1,0:T(8,128)(2,1)} %get-tuple-element.5) | data formatting | bytes 2097152

commit v3 on v2

--- a/solution.py
+++ b/solution.py
@@ -392,7 +392,7 @@
         self.middle = self.tally - self.front - self.back
         self.chunk = 512
         self.steps = self.local // self.chunk
-        self.slots = min(8, self.steps)
+        self.slots = min(4, self.steps)
         self.group = ROW_TILE
         self.snake_rows = 32
         self.send_blocks = 4
@@ -401,7 +401,7 @@
 
 
 def blocks_of(plan):
-    count = 4
+    count = 5
     unit = plan.middle // ROW_TILE
     sizes = [(unit // count + (1 if i < unit % count else 0)) * ROW_TILE for i in range(count)]
     starts = [plan.front + sum(sizes[:i]) for i in range(count)]
@@ -426,8 +426,8 @@
     alpha,
     filters,
     bias,
-    hidden_out,
-    audio_out,
+    hid_v,
+    audio_v,
     q_v,
     nk_v,
     nv_v,
@@ -457,7 +457,6 @@
     o_v,
     out_v,
     in_v,
-    hid_v,
     acc_v,
     sq_v,
     sendc_v,
@@ -468,14 +467,12 @@
     here_v,
     there_v,
     lhs_v,
-    audio_v,
     s_in,
     s_k,
     s_v,
     s_w,
     s_cw,
     s_fw,
-    s_out,
     x_alpha,
     x_head,
     x_early,
@@ -591,6 +588,12 @@
 
     lax.fori_loop(0, steps, start_codec, 0)
 
+    def start_filter(t, carry):
+        filter_in(t).start()
+        return carry
+
+    lax.fori_loop(0, KERNEL_TAPS, start_filter, 0)
+
     for copy in (lens_in, fin_in, own_in):
         copy.wait()
 
@@ -755,11 +758,6 @@
             before_x(m, dp + 1, core).start()
 
 
-    def start_filter(t, carry):
-        filter_in(t).start()
-        return carry
-
-    lax.fori_loop(0, KERNEL_TAPS, start_filter, 0)
     for copy in (res_in, gain_in, bias_in):
         copy.wait()
     gains = gain_raw[...].astype(jnp.float32)
@@ -804,11 +802,11 @@
     weight_in(jnp.int32(steps)).wait()
     part_x(0).wait_recv()
     produce(jnp.int32(0))
+    if slots < steps:
+        weight_in(jnp.int32(steps + slots)).start()
     lax.fori_loop(1, steps, mine_step, 0)
     codec_in(steps - 1).wait()
     consume(jnp.int32(steps - 1))
-    hidden_x = local(hid_v, hidden_out, s_out.at[0])
-    hidden_x.start()
 
     other_cols = pl.ds(pl.multiple_of(other * own, own), own)
     sendc_v[:, :own] = acc_v[:, other_cols]
@@ -882,10 +880,6 @@
 
     for index in range(len(blocks_of(P_))):
         conv_block(index)
-    middle_x = local(
-        audio_v.at[front : tally - back], audio_out.at[front : tally - back], s_out.at[1]
-    )
-    middle_x.start()
 
     alpha_x.wait_recv()
     head_x.wait_recv()
@@ -964,10 +958,6 @@
     audio_v[tally - back :, :] = (edge[front:] + fr_v[tally - back :, :].astype(jnp.float32)).astype(
         jnp.bfloat16
     )
-    first_x = local(audio_v.at[:front], audio_out.at[:front], s_out.at[2])
-    last_x = local(audio_v.at[tally - back :], audio_out.at[tally - back :], s_out.at[3])
-    first_x.start()
-    last_x.start()
 
     alpha_x.wait_send()
     head_x.wait_send()
@@ -1009,10 +999,16 @@
     def _():
         lax.fori_loop(1, count, sent_near, 0)
 
-    hidden_x.wait()
-    middle_x.wait()
-    first_x.wait()
-    last_x.wait()
+
+def store_kernel(hidden, audio, hidden_out, audio_out, sems):
+    copies = (
+        pltpu.make_async_copy(hidden, hidden_out, sems.at[0]),
+        pltpu.make_async_copy(audio, audio_out, sems.at[1]),
+    )
+    for copy in copies:
+        copy.start()
+    for copy in copies:
+        copy.wait()
 
 
 def fused(
@@ -1072,7 +1068,6 @@
         vm((plan.heads, rows, plan.depth), f32),
         vm((plan.steps, rows, plan.chunk), bf),
         vm((plan.steps, rows, plan.chunk), bf),
-        vm((rows, plan.local), bf),
         vm((rows, channels), f32),
         vm((rows, 128), f32),
         vm((rows, own + 128), f32),
@@ -1083,14 +1078,12 @@
         vm((plan.late, channels), f32),
         vm((plan.pad, channels), f32),
         vm((biggest, taps), bf),
-        vm((tally, own), bf),
         dma((11,)),
         dma((plan.heads,)),
         dma((plan.heads,)),
         dma((plan.slots,)),
         dma((plan.steps,)),
         dma((KERNEL_TAPS,)),
-        dma((4,)),
         dma((2,)),
         dma((2,)),
         dma((2, plan.send_blocks)),
@@ -1104,19 +1097,10 @@
         dma((plan.near * n_mp,)),
     ]
     anywhere = pl.BlockSpec(memory_space=pl.ANY)
-    return pl.pallas_call(
-        functools.partial(fused_kernel, plan),
-        out_shape=(
-            jax.ShapeDtypeStruct((rows, plan.local), bf),
-            jax.ShapeDtypeStruct((tally, own), bf),
-        ),
-        in_specs=[anywhere] * 16,
-        out_specs=(anywhere, anywhere),
-        scratch_shapes=scratch,
-        compiler_params=pltpu.CompilerParams(
-            collective_id=1, has_side_effects=True, vmem_limit_bytes=VMEM_BYTES
-        ),
-    )(
+    kept = pl.BlockSpec(memory_space=pltpu.VMEM)
+    operands = [
+        pltpu.with_memory_space_constraint(x, pltpu.HBM)
+        for x in (
         query,
         new_key,
         new_value,
@@ -1133,10 +1117,35 @@
         snake_alpha.reshape(1, -1),
         filter_weight.reshape(taps, own),
         conv_bias.reshape(1, -1),
-    )
-
-
-VMEM_BYTES = 66 * 1000 * 1000
+        )
+    ]
+    kept_pair = pl.pallas_call(
+        functools.partial(fused_kernel, plan),
+        out_shape=(
+            jax.ShapeDtypeStruct((rows, plan.local), bf),
+            jax.ShapeDtypeStruct((tally, own), bf),
+        ),
+        in_specs=[pl.BlockSpec(memory_space=pltpu.HBM)] * 16,
+        out_specs=(kept, kept),
+        scratch_shapes=scratch,
+        compiler_params=pltpu.CompilerParams(
+            collective_id=1, has_side_effects=True, vmem_limit_bytes=VMEM_BYTES
+        ),
+    )(*operands)
+    return pl.pallas_call(
+        store_kernel,
+        out_shape=(
+            jax.ShapeDtypeStruct((rows, plan.local), bf),
+            jax.ShapeDtypeStruct((tally, own), bf),
+        ),
+        in_specs=[kept, kept],
+        out_specs=(anywhere, anywhere),
+        scratch_shapes=[dma((2,))],
+        compiler_params=pltpu.CompilerParams(vmem_limit_bytes=4 * 1024 * 1024),
+    )(*kept_pair)
+
+
+VMEM_BYTES = 48 * 1000 * 1000
 
 
 def step(*args):

time: 40.3 us -> 37.4 us (0.928)
  local copies, waits for them, and re-layouts: 4.13 us -> 0 us
  Pallas kernels: 35.1 us -> 36.4 us
    unnamed x2 -> x0, local copies, waits for them, and re-layouts: 4.13 us -> none
    pallas_call x0 -> x1, Pallas kernels: none -> 1.16 us  [fused(): pl.pallas_call(store_kernel, out_shape=(jax.ShapeDtypeStruct((rows, plan....]
where the time goes in v3:
time: 37.4 us; the launch traced here: 37 us
  Pallas kernels  36.4 us (97%)
  between operations  0.64 us (2%)
    pallas_call x1, Pallas kernels, fused(): pl.pallas_call(functools.partial(fused_kernel, plan), out_shape=(jax.Shap...  35.2 us
    pallas_call x1, Pallas kernels, fused(): pl.pallas_call(store_kernel, out_shape=(jax.ShapeDtypeStruct((rows, plan....  1.16 us

profile of v3, /device:TPU:0, one launch (start us, length us, event | category | flops | bytes accessed | tf_op | source)
XLA Modules:
  0.0 37.0 jit_solution(4631774251002707221)
XLA Ops:
  0.6 35.2 %shard_map.167 = (bf16[64,4096]{1,0:T(8,128)(2,1)S(1)}, bf16[1024,512]{1,0:T(8,128)(2,1)S(1)}) custom-call(bf16[64,2048]{1,0:T(8,128)(2,1)} %query.1, bf16[64,2048]{1,0:T(8,128)(2,1)} %new_key.1, bf16[64,2048]{1,0:T(8,128)(2,1)} %new_value.1, bf16[64,16,16,128]{3,2,1,0:T(8,128)(2,1)} %cache_key.1, bf16[64,16,16,128]{3,2,1,0:T(8,128)(2,1)} %cache_value.1, ...), custom_call_target="tpu_custom_call" | custom-call | tf_op jit(solution)/shard_map/pallas_call | solution.py:1122
  35.8 1.2 %shard_map.168 = (bf16[64,4096]{1,0:T(8,128)(2,1)}, bf16[1024,512]{1,0:T(8,128)(2,1)}) custom-call(bf16[64,4096]{1,0:T(8,128)(2,1)S(1)} %get-tuple-element.4.hidden, bf16[1024,512]{1,0:T(8,128)(2,1)S(1)} %get-tuple-element.5.audio), custom_call_target="tpu_custom_call" | custom-call | tf_op jit(solution)/shard_map/pallas_call | solution.py:1135

commit v4 on v3

--- a/solution.py
+++ b/solution.py
@@ -392,12 +392,13 @@
         self.middle = self.tally - self.front - self.back
         self.chunk = 512
         self.steps = self.local // self.chunk
-        self.slots = min(4, self.steps)
+        self.slots = min(6, self.steps)
         self.group = ROW_TILE
         self.snake_rows = 32
         self.send_blocks = 4
         self.depth_in = self.heads * self.depth
-        self.unroll = 4
+        self.unroll = 8
+        self.octet = 8
 
 
 def blocks_of(plan):
@@ -592,8 +593,6 @@
         filter_in(t).start()
         return carry
 
-    lax.fori_loop(0, KERNEL_TAPS, start_filter, 0)
-
     for copy in (lens_in, fin_in, own_in):
         copy.wait()
 
@@ -620,23 +619,32 @@
     scale = 1.0 / jnp.sqrt(jnp.float32(depth))
 
     def score_step(j, carry):
-        for u in range(P_.unroll):
-            key_in(j * P_.unroll + u).wait()
-        for u in range(P_.unroll):
-            h = j * P_.unroll + u
-            cols = pl.ds(pl.multiple_of(h * depth, depth), depth)
-            for g in range(rows // P_.group):
-                part = slice(g * P_.group, (g + 1) * P_.group)
-                keys = k_v[h, part].reshape(lanes, depth)
-                score_v[h, part, :] = lax.dot_general(
-                    q_v[part, cols],
-                    keys,
-                    (((1,), (1,)), ((), ())),
-                    preferred_element_type=jnp.float32,
-                )
-        return carry
-
-    lax.fori_loop(0, heads // P_.unroll, score_step, 0)
+        for u in range(P_.octet):
+            key_in(j * P_.octet + u).wait()
+        lane_head = iota((depth, P_.octet * P_.group), 1) // P_.group
+        for g in range(rows // P_.group):
+            part = slice(g * P_.group, (g + 1) * P_.group)
+            stacked, keys = [], []
+            for u in range(P_.octet):
+                h = j * P_.octet + u
+                cols = pl.ds(pl.multiple_of(h * depth, depth), depth)
+                stacked.append(q_v[part, cols].astype(jnp.float32))
+                keys.append(k_v[h, part].reshape(lanes, depth))
+            turned = jnp.concatenate(stacked, axis=0).T
+            queries = [
+                jnp.where(lane_head == u, turned, 0.0).astype(jnp.bfloat16)
+                for u in range(P_.octet)
+            ]
+            found = jnp.dot(
+                jnp.concatenate(keys, axis=1),
+                jnp.concatenate(queries, axis=0),
+                preferred_element_type=jnp.float32,
+            ).T
+            for u in range(P_.octet):
+                score_v[j * P_.octet + u, part, :] = found[u * P_.group : (u + 1) * P_.group]
+        return carry
+
+    lax.fori_loop(0, heads // P_.octet, score_step, 0)
 
     def soft_step(h, carry):
         cols = pl.ds(pl.multiple_of(h * depth, depth), depth)
@@ -717,6 +725,7 @@
         for m in range(n_mp):
             after_x(m, dp - 1, core).start()
 
+
     for copy in (alpha_in, frames_in):
         copy.wait()
     my_alpha = al_v[:, mine_cols]
@@ -748,7 +757,6 @@
 
     lax.fori_loop(0, steps, their_step, 0)
     part_x(steps - 1).start()
-
     for b in range(P_.send_blocks):
         early_x(b).start()
 
@@ -766,9 +774,11 @@
     acc_v[...] = jnp.zeros_like(acc_v)
     sq_v[...] = jnp.zeros_like(sq_v)
 
-    def produce(i):
+    def produce(i, first=False):
         cols = pl.ds(pl.multiple_of(i * chunk, chunk), chunk)
-        total = jnp.dot(att_v[...], w_v[lax.rem(i, slots)], preferred_element_type=jnp.float32)
+        total = jnp.dot(att_v[...], w_v[lax.rem(i + steps, slots)], preferred_element_type=jnp.float32)
+        if first:
+            part_x(0).wait_recv()
         total = total + in_v[i].astype(jnp.float32) + res_v[:, cols].astype(jnp.float32)
         hidden = total.astype(jnp.bfloat16)
         hid_v[:, cols] = hidden
@@ -797,11 +807,14 @@
         def _():
             weight_in(i + steps + slots).start()
 
+        @pl.when(i == max(1, steps - slots))
+        def _():
+            lax.fori_loop(0, KERNEL_TAPS, start_filter, 0)
+
         return carry
 
     weight_in(jnp.int32(steps)).wait()
-    part_x(0).wait_recv()
-    produce(jnp.int32(0))
+    produce(jnp.int32(0), True)
     if slots < steps:
         weight_in(jnp.int32(steps + slots)).start()
     lax.fori_loop(1, steps, mine_step, 0)
@@ -884,34 +897,83 @@
     alpha_x.wait_recv()
     head_x.wait_recv()
 
-    def finish(step, carry):
-        peer, pd, pm = place(step)
-        copy_a(pd, pm, pd, pm, peer, peer).wait_recv()
-        return carry
-
-    lax.fori_loop(1, count, finish, 0)
-    for s in range(n_dp):
-        for m in range(n_mp):
-            here_v[s * CAP : (s + 1) * CAP, m * own : (m + 1) * own] = land_v[m, s].astype(
-                jnp.float32
-            )
-    for b in range(P_.send_blocks):
-        early_x(b).wait_send()
-    hf = hf_v[...].astype(jnp.float32)
-    mf = fr_v[0:late, :].astype(jnp.float32)
-
     all_alpha = al_v[...]
     all_turn = all_alpha * 0.3183098861837907
     all_inverse = 1.0 / all_alpha
-    here_v[:, mine_cols] += mf
-    here_v[:, other_cols] += hf
-    act_v[pad : pad + late, :] = fast_snake(here_v[...], all_alpha, all_turn, all_inverse)
+    here_v[:, mine_cols] = fr_v[0:late, :].astype(jnp.float32)
+    here_v[:, other_cols] = hf_v[...].astype(jnp.float32)
 
     @pl.when(dp < n_dp - 1)
     def _():
         for m in range(n_mp):
             after_x(0, 0, m).wait_recv()
-
+            there_v[:, m * own : (m + 1) * own] = af_v[m].astype(jnp.float32)
+
+    for b in range(P_.send_blocks):
+        early_x(b).wait_send()
+    @pl.when(dp > 0)
+    def _():
+        for m in range(n_mp):
+            before_x(0, 0, m).wait_recv()
+
+    @pl.when(dp == 0)
+    def _():
+        act_v[0:pad, :] = jnp.zeros((pad, channels), jnp.bfloat16)
+
+    alpha_x.wait_send()
+    head_x.wait_send()
+
+    @pl.when(dp < n_dp - 1)
+    def _():
+        for m in range(n_mp):
+            before_x(m, 0, core).wait_send()
+
+    @pl.when(dp > 0)
+    def _():
+        for m in range(n_mp):
+            after_x(m, 0, core).wait_send()
+
+    def part_sent(i, carry):
+        part_x(i).wait_send()
+        return carry
+
+    lax.fori_loop(0, steps, part_sent, 0)
+    codec_x.wait_send()
+
+    def sent(step, carry):
+        peer, pd, pm = place(step)
+        copy_a(pd, pm, dp, core, peer, me).wait_send()
+        return carry
+
+    lax.fori_loop(1, count, sent, 0)
+
+    def sent_near(step, carry):
+        peer, pd, pm = place(step)
+
+        @pl.when(pd < n_dp - 1)
+        def _():
+            copy_b(pd, pm, dp, core, peer, me).wait_send()
+
+        return carry
+
+    @pl.when(dp < P_.near)
+    def _():
+        lax.fori_loop(1, count, sent_near, 0)
+
+    for s in range(n_dp):
+        for m in range(n_mp):
+
+            @pl.when(me != s * n_mp + m)
+            def _(s=s, m=m):
+                copy_a(0, 0, s, m, 0, s * n_mp + m).wait_recv()
+
+            here_v[s * CAP : (s + 1) * CAP, m * own : (m + 1) * own] += land_v[m, s].astype(
+                jnp.float32
+            )
+    act_v[pad : pad + late, :] = fast_snake(here_v[...], all_alpha, all_turn, all_inverse)
+
+    @pl.when(dp < n_dp - 1)
+    def _():
         def take_near(sender, carry):
             @pl.when(sender != me)
             def _():
@@ -921,7 +983,6 @@
 
         lax.fori_loop(0, P_.near * n_mp, take_near, 0)
         for m in range(n_mp):
-            there_v[:, m * own : (m + 1) * own] = af_v[m].astype(jnp.float32)
             for s in range(P_.near):
                 there_v[s * CAP : (s + 1) * CAP, m * own : (m + 1) * own] += near_v[m, s].astype(
                     jnp.float32
@@ -931,15 +992,6 @@
     @pl.when(dp == n_dp - 1)
     def _():
         act_v[pad + tally :, :] = jnp.zeros((pad, channels), jnp.bfloat16)
-
-    @pl.when(dp > 0)
-    def _():
-        for m in range(n_mp):
-            before_x(0, 0, m).wait_recv()
-
-    @pl.when(dp == 0)
-    def _():
-        act_v[0:pad, :] = jnp.zeros((pad, channels), jnp.bfloat16)
 
     for t in range(KERNEL_TAPS):
         cols = slice(t * channels, (t + 1) * channels)
@@ -958,46 +1010,6 @@
     audio_v[tally - back :, :] = (edge[front:] + fr_v[tally - back :, :].astype(jnp.float32)).astype(
         jnp.bfloat16
     )
-
-    alpha_x.wait_send()
-    head_x.wait_send()
-
-    @pl.when(dp < n_dp - 1)
-    def _():
-        for m in range(n_mp):
-            before_x(m, 0, core).wait_send()
-
-    @pl.when(dp > 0)
-    def _():
-        for m in range(n_mp):
-            after_x(m, 0, core).wait_send()
-
-    def part_sent(i, carry):
-        part_x(i).wait_send()
-        return carry
-
-    lax.fori_loop(0, steps, part_sent, 0)
-    codec_x.wait_send()
-
-    def sent(step, carry):
-        peer, pd, pm = place(step)
-        copy_a(pd, pm, dp, core, peer, me).wait_send()
-        return carry
-
-    lax.fori_loop(1, count, sent, 0)
-
-    def sent_near(step, carry):
-        peer, pd, pm = place(step)
-
-        @pl.when(pd < n_dp - 1)
-        def _():
-            copy_b(pd, pm, dp, core, peer, me).wait_send()
-
-        return carry
-
-    @pl.when(dp < P_.near)
-    def _():
-        lax.fori_loop(1, count, sent_near, 0)
 
 
 def store_kernel(hidden, audio, hidden_out, audio_out, sems):
@@ -1145,7 +1157,7 @@
     )(*kept_pair)
 
 
-VMEM_BYTES = 48 * 1000 * 1000
+VMEM_BYTES = 53 * 1000 * 1000
 
 
 def step(*args):

time: 37.4 us -> 37.1 us (level)
  no operation moved by 1% of the time
where the time goes in v4:
time: 37.1 us; the launch traced here: 36.7 us
  Pallas kernels  36.1 us (97%)
  between operations  0.64 us (2%)
    pallas_call x1, Pallas kernels, fused(): pl.pallas_call(functools.partial(fused_kernel, plan), out_shape=(jax.Shap...  34.9 us
    pallas_call x1, Pallas kernels, fused(): pl.pallas_call(store_kernel, out_shape=(jax.ShapeDtypeStruct((rows, plan....  1.16 us

profile of v4, /device:TPU:0, one launch (start us, length us, event | category | flops | bytes accessed | tf_op | source)
XLA Modules:
  0.0 36.7 jit_solution(12186600734363393404)
XLA Ops:
  0.6 34.9 %shard_map.167 = (bf16[64,4096]{1,0:T(8,128)(2,1)S(1)}, bf16[1024,512]{1,0:T(8,128)(2,1)S(1)}) custom-call(bf16[64,2048]{1,0:T(8,128)(2,1)} %query.1, bf16[64,2048]{1,0:T(8,128)(2,1)} %new_key.1, bf16[64,2048]{1,0:T(8,128)(2,1)} %new_value.1, bf16[64,16,16,128]{3,2,1,0:T(8,128)(2,1)} %cache_key.1, bf16[64,16,16,128]{3,2,1,0:T(8,128)(2,1)} %cache_value.1, ...), custom_call_target="tpu_custom_call" | custom-call | tf_op jit(solution)/shard_map/pallas_call | solution.py:1134
  35.6 1.2 %shard_map.168 = (bf16[64,4096]{1,0:T(8,128)(2,1)}, bf16[1024,512]{1,0:T(8,128)(2,1)}) custom-call(bf16[64,4096]{1,0:T(8,128)(2,1)S(1)} %get-tuple-element.4.hidden, bf16[1024,512]{1,0:T(8,128)(2,1)S(1)} %get-tuple-element.5.audio), custom_call_target="tpu_custom_call" | custom-call | tf_op jit(solution)/shard_map/pallas_call | solution.py:1147

commit v5 on v4

--- a/solution.py
+++ b/solution.py
@@ -871,11 +871,11 @@
         copy_a(pd, pm, dp, core, peer, me).start()
         return carry
 
-    lax.fori_loop(1, count, send, 0)
+    lax.fori_loop(1, count, send, 0, unroll=True)
 
     @pl.when(dp < P_.near)
     def _():
-        lax.fori_loop(1, count, send_near, 0)
+        lax.fori_loop(1, count, send_near, 0, unroll=True)
 
     land_v[core, dp] = sendh_v[dp]
 

time: 37.1 us -> 36.3 us (0.978)
  Pallas kernels: 36.1 us -> 35.3 us
    pallas_call x1, Pallas kernels: 34.9 us -> 34.1 us  [fused(): pl.pallas_call(functools.partial(fused_kernel, plan), out_shape=(jax.Shap...]
where the time goes in v5:
time: 36.3 us; the launch traced here: 35.9 us
  Pallas kernels  35.3 us (97%)
  between operations  0.64 us (2%)
    pallas_call x1, Pallas kernels, fused(): pl.pallas_call(functools.partial(fused_kernel, plan), out_shape=(jax.Shap...  34.1 us
    pallas_call x1, Pallas kernels, fused(): pl.pallas_call(store_kernel, out_shape=(jax.ShapeDtypeStruct((rows, plan....  1.16 us

profile of v5, /device:TPU:0, one launch (start us, length us, event | category | flops | bytes accessed | tf_op | source)
XLA Modules:
  0.0 35.9 jit_solution(11927743161133981891)
XLA Ops:
  0.6 34.1 %shard_map.167 = (bf16[64,4096]{1,0:T(8,128)(2,1)S(1)}, bf16[1024,512]{1,0:T(8,128)(2,1)S(1)}) custom-call(bf16[64,2048]{1,0:T(8,128)(2,1)} %query.1, bf16[64,2048]{1,0:T(8,128)(2,1)} %new_key.1, bf16[64,2048]{1,0:T(8,128)(2,1)} %new_value.1, bf16[64,16,16,128]{3,2,1,0:T(8,128)(2,1)} %cache_key.1, bf16[64,16,16,128]{3,2,1,0:T(8,128)(2,1)} %cache_value.1, ...), custom_call_target="tpu_custom_call" | custom-call | tf_op jit(solution)/shard_map/pallas_call | solution.py:1134
  34.7 1.2 %shard_map.168 = (bf16[64,4096]{1,0:T(8,128)(2,1)}, bf16[1024,512]{1,0:T(8,128)(2,1)}) custom-call(bf16[64,4096]{1,0:T(8,128)(2,1)S(1)} %get-tuple-element.4.hidden, bf16[1024,512]{1,0:T(8,128)(2,1)S(1)} %get-tuple-element.5.audio), custom_call_target="tpu_custom_call" | custom-call | tf_op jit(solution)/shard_map/pallas_call | solution.py:1147
